TPU v7x, 256 devices: a whole 4x4x8 slice. The times are simulated.
256 devices in a mesh: mem: 128 (over z, x, y), tp: 2 (over core).
Axes of the slice: x: 4, y: 4, z: 8, core: 2. Of those that a mesh axis runs over, the one named last changes fastest.
Arguments:
- queries: bfloat16 [65536, 2048], P('mem', 'tp')
- local_keys: bfloat16 [65536, 2048], P('mem', 'tp')
- local_values: bfloat16 [65536, 2048], P('mem', 'tp'), may hold values from -6 to 6
- mem_keys: bfloat16 [131072, 2048], P('mem', 'tp')
- mem_values: bfloat16 [131072, 2048], P('mem', 'tp'), may hold values from -6 to 6
- gate_bias: float32 [16], P('tp'), may hold values from -2 to 2
- out_weight: bfloat16 [2048, 2048], P('tp'), may hold values from -0.125 to 0.125
- block_ids: int32 [128, 16, 16], replicated, may hold values from 0 to 1023, as said below
- block_home: int32 [1024], replicated, may hold values from 0 to 1023, as said below
Outputs:
- mixed: bfloat16 [65536, 2048], P(('mem', 'tp'))
Inputs may be any that keep to these rules, and one draw needn't show every extreme that they name: `block_ids`: block_home is a permutation of the block ids. Let the holder of a block b be block_home[b] // 8. For each sequence block and each group of 8 heads starting at a multiple of 8, at most 2 of the group's 8 * 16 listed entries have the same holder, and some holder has exactly 2 of them. Ids may repeat within a list. `block_home`: A permutation of the block ids.
All inputs are finite; a program needn't handle non-finite values.
Results may differ from a plain program's by a relative error of at most 0.0057.
Values may be sent and summed in bfloat16 or wider, within the bound.
A program may use at most 128 MiB of HBM per device.

v0:
```python
import math

import jax
import jax.numpy as jnp
from jax import lax
from jax.sharding import PartitionSpec as P

HD = 128
BLK = 128
TOPK = 16


def attend(query_head, key_rows, value_rows, factor, visible):
    scores = (
        lax.dot_general(
            query_head, key_rows, (((1,), (1,)), ((), ())), preferred_element_type=jnp.float32
        )
        * factor
    )
    if visible is not None:
        scores = jnp.where(visible, scores, -1e30)
    highest = jnp.max(scores, axis=1, keepdims=True)
    exponent = jnp.exp(scores - highest)
    weights = (exponent / jnp.sum(exponent, axis=1, keepdims=True)).astype(jnp.bfloat16)
    return jnp.dot(weights, value_rows, preferred_element_type=jnp.float32)


def rank_within(owner_row):
    request_count = owner_row.shape[0]
    order_index = jnp.arange(request_count, dtype=jnp.int32)
    earlier = order_index[:, None] > order_index[None, :]
    same_owner = owner_row[:, None] == owner_row[None, :]
    return jnp.sum((same_owner & earlier).astype(jnp.int32), axis=1)


def per_device(
    queries,
    local_keys,
    local_values,
    mem_keys,
    mem_values,
    gate_bias,
    out_weight,
    block_ids,
    block_home,
):
    mem_count = lax.axis_size("mem")
    mem_index = lax.axis_index("mem")
    tp_index = lax.axis_index("tp")
    head_count = queries.shape[1] // HD
    span_rows = queries.shape[0]
    blocks_here = mem_keys.shape[0] // BLK
    request_count = head_count * TOPK
    slot_count = max(2, 2 * request_count // mem_count)
    group_ids = lax.dynamic_slice_in_dim(block_ids, tp_index * head_count, head_count, 1)
    group_ids = group_ids.reshape(mem_count, request_count)
    home_slots = jnp.take(block_home, group_ids, axis=0)
    owners = home_slots // blocks_here
    local_block = home_slots % blocks_here
    head_of_request = jnp.arange(request_count, dtype=jnp.int32) // TOPK
    request_codes = local_block * head_count + head_of_request[None, :]
    own_owners = lax.dynamic_index_in_dim(owners, mem_index, 0, keepdims=False)
    own_codes = lax.dynamic_index_in_dim(request_codes, mem_index, 0, keepdims=False)
    own_ranks = rank_within(own_owners)
    slot_index = jnp.arange(slot_count, dtype=jnp.int32)
    owner_index = jnp.arange(mem_count, dtype=jnp.int32)
    matches = (own_owners[None, None, :] == owner_index[:, None, None]) & (
        own_ranks[None, None, :] == slot_index[None, :, None]
    )
    table = jnp.sum(jnp.where(matches, own_codes[None, None, :], 0), axis=2)
    wanted = lax.all_to_all(table, "mem", split_axis=0, concat_axis=0, tiled=True)
    key_blocks = mem_keys.reshape(blocks_here, BLK, head_count, HD)
    value_blocks = mem_values.reshape(blocks_here, BLK, head_count, HD)
    chosen_block = wanted // head_count
    chosen_head = wanted % head_count
    sent_keys = key_blocks[chosen_block, :, chosen_head, :]
    sent_values = value_blocks[chosen_block, :, chosen_head, :]
    got_keys, got_values = (
        lax.all_to_all(sent_keys, "mem", split_axis=0, concat_axis=0, tiled=True),
        lax.all_to_all(sent_values, "mem", split_axis=0, concat_axis=0, tiled=True),
    )
    flat_slot = own_owners * slot_count + own_ranks
    far_keys = jnp.take(got_keys.reshape(mem_count * slot_count, BLK, HD), flat_slot, axis=0)
    far_keys = far_keys.reshape(head_count, TOPK * BLK, HD)
    far_values = jnp.take(got_values.reshape(mem_count * slot_count, BLK, HD), flat_slot, axis=0)
    far_values = far_values.reshape(head_count, TOPK * BLK, HD)
    factor = 1.0 / math.sqrt(HD)
    positions = jnp.arange(span_rows, dtype=jnp.int32)
    causal = positions[:, None] >= positions[None, :]
    mixing = jax.nn.sigmoid(gate_bias)
    outputs = []
    for head_number in range(head_count):
        low_column = head_number * HD
        query_head = queries[:, low_column : low_column + HD]
        remote = attend(query_head, far_keys[head_number], far_values[head_number], factor, None)
        nearby = attend(
            query_head,
            local_keys[:, low_column : low_column + HD],
            local_values[:, low_column : low_column + HD],
            factor,
            causal,
        )
        outputs.append(mixing[head_number] * remote + (1.0 - mixing[head_number]) * nearby)
    combined = jnp.concatenate(outputs, axis=1).astype(jnp.bfloat16)
    mixed = lax.psum_scatter(
        jnp.dot(combined, out_weight, preferred_element_type=jnp.float32),
        "tp",
        scatter_dimension=0,
        tiled=True,
    )
    return mixed.astype(jnp.bfloat16)


def solution(mesh):
    in_specs = (
        P("mem", "tp"),
        P("mem", "tp"),
        P("mem", "tp"),
        P("mem", "tp"),
        P("mem", "tp"),
        P("tp"),
        P("tp", None),
        P(),
        P(),
    )
    out_specs = P(("mem", "tp"), None)
    return jax.shard_map(
        per_device, mesh=mesh, in_specs=in_specs, out_specs=out_specs, check_vma=False
    )
```

profile of v0, /device:TPU:1, one launch (start us, length us, event | category | flops | bytes accessed | tf_op | source)
XLA Modules:
  0.0 570.7 jit_solution(17227145754059411136)
XLA Ops:
  6.5 0.9 copy-done
  7.6 65.3 %gather_fusion = s32[16384]{0:T(1024)S(1)} fusion(s32[1024]{0:T(1024)S(1)} %copy-done.2, s32[16384]{0:T(1024)S(1)} %bitcast_clamp_fusion), kind=kCustom, calls=%fused_computation.2 | custom fusion | bytes 196608 | tf_op jit(solution)/shard_map/jit(_take)/gather | solution.py:57
  73.6 0.7 copy.24
  74.4 16.3 %all-to-all-start = ((s32[128,1,2]{2,1,0:T(1,128)}), s32[128,1,2]{2,1,0:T(1,128)S(1)}, u32[]{:S(2)}, u32[]{:S(2)}) async-start(s32[128,1,2]{2,1,0:T(1,128)} %copy.24), calls=%async_computation | async-start | bytes 131072 | tf_op jit(solution)/shard_map/all_to_all | solution.py:71
  91.9 9.5 %all-to-all-done = s32[128,1,2]{2,1,0:T(1,128)S(1)} async-done(((s32[128,1,2]{2,1,0:T(1,128)}), s32[128,1,2]{2,1,0:T(1,128)S(1)}, u32[]{:S(2)}, u32[]{:S(2)}) %all-to-all-start) | async-done | bytes 1056 | tf_op jit(solution)/shard_map/all_to_all | solution.py:71
  101.7 9.8 %gather_fusion.1 = bf16[256,128,128]{2,1,0:T(8,128)(2,1)} fusion(bf16[8,128,8,128]{3,1,2,0:T(8,128)(2,1)S(1)} %copy.27, s32[256]{0:T(256)S(1)} %reshape.340), kind=kCustom, calls=%fused_computation.3 | custom fusion | bytes 16779264 | tf_op jit(solution)/shard_map/gather | solution.py:76
  111.5 7.8 %all-to-all-start.1 = ((bf16[128,2,128,128]{3,2,1,0:T(8,128)(2,1)}), bf16[128,2,128,128]{3,2,1,0:T(8,128)(2,1)}, u32[]{:S(2)}, u32[]{:S(2)}) async-start(bf16[128,2,128,128]{3,2,1,0:T(8,128)(2,1)} %bitcast.80), calls=%async_computation.1 | async-start | bytes 16777216 | tf_op jit(solution)/shard_map/all_to_all | solution.py:79
  120.6 9.8 %gather_fusion.2 = bf16[256,128,128]{2,1,0:T(8,128)(2,1)} fusion(bf16[8,128,8,128]{3,1,2,0:T(8,128)(2,1)S(1)} %copy.28, s32[256]{0:T(256)S(1)} %reshape.340), kind=kCustom, calls=%fused_computation.4 | custom fusion | bytes 16779264 | tf_op jit(solution)/shard_map/gather | solution.py:77
  130.4 169.9 %all-to-all-done.1 = bf16[128,2,128,128]{3,2,1,0:T(8,128)(2,1)} async-done(((bf16[128,2,128,128]{3,2,1,0:T(8,128)(2,1)}), bf16[128,2,128,128]{3,2,1,0:T(8,128)(2,1)}, u32[]{:S(2)}, u32[]{:S(2)}) %all-to-all-start.1) | async-done | bytes 8388640 | tf_op jit(solution)/shard_map/all_to_all | solution.py:79
  300.3 13.3 %all-to-all-start.2 = ((bf16[128,2,128,128]{3,2,1,0:T(8,128)(2,1)}), bf16[128,2,128,128]{3,2,1,0:T(8,128)(2,1)}, u32[]{:S(2)}, u32[]{:S(2)}) async-start(bf16[128,2,128,128]{3,2,1,0:T(8,128)(2,1)} %bitcast.79), calls=%async_computation.2 | async-start | bytes 16777216 | tf_op jit(solution)/shard_map/all_to_all | solution.py:80
  319.4 1.3 fusion.141
  320.7 1.0 copy-done.15
  321.8 1.3 fusion.142
  323.1 1.0 copy-done.13
  324.4 1.3 fusion.143
  325.7 1.0 copy-done.11
  326.8 1.3 fusion.144
  328.1 1.0 copy-done.9
  329.3 1.3 fusion.145
  330.8 1.5 fusion.146
  332.4 1.3 fusion.147
  333.9 1.3 fusion.148
  335.4 6.4 %gather_fusion.3 = bf16[128,128,128]{2,1,0:T(8,128)(2,1)} fusion(bf16[256,128,128]{2,1,0:T(8,128)(2,1)} %bitcast.8, s32[1024]{0:T(1024)S(1)} %pad_clamp_fusion), kind=kCustom, calls=%fused_computation.clone | custom fusion | bytes 8389120 | tf_op jit(solution)/shard_map/jit(_take)/gather | solution.py:83
  341.9 151.9 %all-to-all-done.2 = bf16[128,2,128,128]{3,2,1,0:T(8,128)(2,1)} async-done(((bf16[128,2,128,128]{3,2,1,0:T(8,128)(2,1)}), bf16[128,2,128,128]{3,2,1,0:T(8,128)(2,1)}, u32[]{:S(2)}, u32[]{:S(2)}) %all-to-all-start.2) | async-done | bytes 8388640 | tf_op jit(solution)/shard_map/all_to_all | solution.py:80
  493.8 6.4 %gather_fusion.4 = bf16[128,128,128]{2,1,0:T(8,128)(2,1)} fusion(bf16[256,128,128]{2,1,0:T(8,128)(2,1)} %bitcast.11, s32[1024]{0:T(1024)S(1)} %pad_clamp_fusion), kind=kCustom, calls=%fused_computation.1.clone | custom fusion | bytes 8389120 | tf_op jit(solution)/shard_map/jit(_take)/gather | solution.py:85
  500.2 4.0 broadcast_select_fusion.1
  504.2 1.0 fusion.138
  511.3 0.8 fusion
  512.1 1.6 fusion.39
  513.7 0.8 fusion.1
  514.4 1.5 fusion.38
  516.0 0.8 fusion.2
  516.7 1.6 fusion.37
  518.4 0.8 fusion.3
  519.1 1.8 fusion.36
  520.9 0.8 fusion.4
  521.7 1.6 fusion.35
  523.3 0.8 fusion.5
  524.1 1.7 fusion.34
  525.7 0.8 fusion.6
  526.5 1.6 fusion.33
  528.1 0.8 fusion.7
  528.9 1.8 fusion.32
  531.1 0.8 copy-done.14
  535.1 1.4 copy-done.3
  536.5 4.4 fusion.149
  540.9 19.8 %reduce-scatter.2.cloned.1.call-done = f32[256,2048]{1,0:T(8,128)} async-done(((f32[512,2048]{1,0:T(8,128)}), f32[256,2048]{1,0:T(8,128)}) %reduce-scatter.2.cloned.1.call-update) | async-done | bytes 2097168 | tf_op jit(solution)/shard_map/reduce_scatter | solution.py:105
  560.7 2.7 convert_element_type.48
  (81 shorter events, 15.5 us)
Async XLA Ops:
  6.5 0.9 copy-start
  6.5 1.0 copy-start.2
  7.6 83.1 %copy-start.4 = (bf16[1024,1024]{1,0:T(8,128)(2,1)S(1)}, bf16[1024,1024]{1,0:T(8,128)(2,1)}, u32[]{:S(2)}) copy-start(bf16[1024,1024]{1,0:T(8,128)(2,1)} %param.14) | copy-start | bytes 6291460
  74.4 27.0 %all-to-all-start = ((s32[128,1,2]{2,1,0:T(1,128)}), s32[128,1,2]{2,1,0:T(1,128)S(1)}, u32[]{:S(2)}, u32[]{:S(2)}) async-start(s32[128,1,2]{2,1,0:T(1,128)} %copy.24), calls=%async_computation | async-start | bytes 131072 | tf_op jit(solution)/shard_map/all_to_all | solution.py:71
  111.5 7.8 %copy-start.5 = (bf16[1024,1024]{1,0:T(8,128)(2,1)S(1)}, bf16[1024,1024]{1,0:T(8,128)(2,1)}, u32[]{:S(2)}) copy-start(bf16[1024,1024]{1,0:T(8,128)(2,1)} %param.15) | copy-start | bytes 6291460
  111.5 188.7 %all-to-all-start.1 = ((bf16[128,2,128,128]{3,2,1,0:T(8,128)(2,1)}), bf16[128,2,128,128]{3,2,1,0:T(8,128)(2,1)}, u32[]{:S(2)}, u32[]{:S(2)}) async-start(bf16[128,2,128,128]{3,2,1,0:T(8,128)(2,1)} %bitcast.80), calls=%async_computation.1 | async-start | bytes 16777216 | tf_op jit(solution)/shard_map/all_to_all | solution.py:79
  300.3 13.4 %copy-start.18 = (f32[8]{0:T(128)S(1)}, f32[8]{0:T(128)}, u32[]{:S(2)}) copy-start(f32[8]{0:T(128)} %param.16) | copy-start | bytes 100
  300.3 193.5 %all-to-all-start.2 = ((bf16[128,2,128,128]{3,2,1,0:T(8,128)(2,1)}), bf16[128,2,128,128]{3,2,1,0:T(8,128)(2,1)}, u32[]{:S(2)}, u32[]{:S(2)}) async-start(bf16[128,2,128,128]{3,2,1,0:T(8,128)(2,1)} %bitcast.79), calls=%async_computation.2 | async-start | bytes 16777216 | tf_op jit(solution)/shard_map/all_to_all | solution.py:80
  313.6 247.0 %reduce-scatter.2.cloned.1.call-start = ((), (), s32[]{:S(2)}) async-start(), calls=%async_computation.4 | async-start | bytes 6291456 | tf_op jit(solution)/shard_map/reduce_scatter | solution.py:105
  320.7 1.0 copy-start.15
  323.1 1.1 copy-start.13
  325.6 1.0 copy-start.11
  328.1 1.0 copy-start.9
  330.6 4.9 copy-start.7
  504.2 1.2 copy-start.6
  528.9 1.8 copy-start.16
  528.9 1.8 copy-start.17
  530.7 1.2 copy-start.14
  530.7 1.6 copy-start.12
  531.9 1.3 copy-start.10
  532.3 1.3 copy-start.8
  534.3 2.2 copy-start.3
  536.5 26.9 %copy-start.1 = (s32[128,16,16]{0,2,1:T(8,128)S(1)}, s32[128,16,16]{0,2,1:T(8,128)}, u32[]{:S(2)}) copy-start(s32[128,16,16]{0,2,1:T(8,128)} %param.18) | copy-start | bytes 393220
Sparse Core Ops, SparseCore 0:
  541.0 19.5 reduce-scatter.1
where the time goes:
time: 578 us; the launch traced here: 571 us
  waiting for transfers between devices  351 us (61%)
  local copies, waits for them, and re-layouts  111 us (19%)
  starting transfers between devices  37.5 us (6%)
  matrix products  36.8 us (6%)
  between operations  19.2 us (3%)
  other arithmetic  15.1 us (3%)
    all_to_all x1, waiting for transfers between devices, per_device(): lax.all_to_all(sent_keys, 'mem', split_axis=0, concat_axis=0, tiled=True)  170 us
    all_to_all x1, waiting for transfers between devices, per_device(): lax.all_to_all(sent_values, 'mem', split_axis=0, concat_axis=0, tiled=True)  152 us
    gather x2, local copies, waits for them, and re-layouts, per_device(): home_slots = jnp.take(block_home, group_ids, axis=0)  65.4 us
    reduce_scatter x1, waiting for transfers between devices, per_device(): lax.psum_scatter(jnp.dot(combined, out_weight, preferred_element_type=jnp...  19.8 us
    all_to_all x1, starting transfers between devices, per_device(): lax.all_to_all(table, 'mem', split_axis=0, concat_axis=0, tiled=True)  16.3 us
    dot_general x16, matrix products, attend(): lax.dot_general(query_head, key_rows, (((1,), (1,)), ((), ())), preferred...  16.3 us
    dot_general x16, matrix products, attend(): return jnp.dot(weights, value_rows, preferred_element_type=jnp.float32)  16.1 us
    all_to_all x1, starting transfers between devices, per_device(): lax.all_to_all(sent_values, 'mem', split_axis=0, concat_axis=0, tiled=True)  13.3 us
  transfers between devices with their start and end apart: 4, of which 4 were waited for; matrix products, arithmetic and copies ran while one was open for 6% of the time, Pallas kernels for 0%

commit v1 on v0

v1 whole, which is shorter than its diff:
```python
import functools
import math

import jax
import jax.numpy as jnp
from jax import lax
from jax.experimental import pallas as pl
from jax.experimental.pallas import tpu as pltpu
from jax.sharding import PartitionSpec as P

HD = 128
BLK = 128
TOPK = 16
PLANES = 8
SIDE = 16
HL = 8
GROUPS = 2
HG = HL // GROUPS
MB = 8
ROWS = BLK // SIDE
OWN = SIDE * MB * HG
CAPS = (344, 280, 200, 88)
OFFS = (0, 344, 624, 824)
CSUM = 912
NPIECE = OWN + 2 * CSUM
LPAD = 384
SLOTS = HG * TOPK
MESH = pl.DeviceIdType.MESH
F32 = jnp.float32
BF16 = jnp.bfloat16
SCALE = math.log2(math.e) / math.sqrt(HD)


def iota(shape, axis):
    return lax.broadcasted_iota(jnp.int32, shape, axis)


def hot(mask):
    return jnp.where(mask, 1.0, 0.0).astype(BF16)


def dot(a, b, dims):
    return lax.dot_general(a, b, (dims, ((), ())), preferred_element_type=F32)


def ways(dz, even):
    up = ((dz >= 1) & (dz <= 3)) | ((dz == 4) & even)
    down = (dz >= 5) | ((dz == 4) & jnp.logical_not(even))
    return up, down


def plan_kernel(plane_ref, ids_ref, home_ref, lists_ref, dest_ref, ok_ref, need, hi_s, code_s, rank_s):
    lane = iota((1, 2048), 1)
    head = (lane >> 4) & 7
    head_term = (head >> 2) * 128 + (head & 3) * 8

    def one_row(row, carry):
        ids = ids_ref[pl.ds(row, 1), :]
        by_hi = hot(iota((32, 2048), 0) == (ids >> 5))
        both = dot(home_ref[...], by_hi, ((1,), (0,)))
        at_lo = iota((32, 2048), 0) == (ids & 31)
        pos_hi = jnp.sum(jnp.where(at_lo, both[:32], 0.0), axis=0, keepdims=True).astype(jnp.int32)
        pos_lo = jnp.sum(jnp.where(at_lo, both[32:], 0.0), axis=0, keepdims=True).astype(jnp.int32)
        code = (pos_lo >> 3) * 32 + head_term + (pos_lo & 7)
        count = dot(
            hot(iota((32, 2048), 0) == pos_hi), hot(iota((256, 2048), 0) == code), ((1,), (1,))
        )
        need[row] = count
        hi_s[pl.ds(row, 1), :] = pos_hi
        code_s[pl.ds(row, 1), :] = code
        return carry

    lax.fori_loop(0, 16, one_row, 0)

    row_plane = iota((32, 256), 0) >> 2
    even = (iota((32, 256), 1) & 1) == 0
    r, s = iota((256, 256), 0), iota((256, 256), 1)
    same_group = (r >> 7) == (s >> 7)
    prefix = hot(same_group & (r <= s))
    whole = hot(same_group)
    same_plane = (r >> 2) == (s >> 2)
    rows_before = hot(same_plane & (s < r))
    rows_all = hot(same_plane)
    over = jnp.zeros((32, 256), F32)
    ranks_all = []
    for side in range(2):
        far = [jnp.zeros((32, 256), jnp.int32), jnp.zeros((32, 256), jnp.int32)]
        for zr in range(PLANES):
            wanted = need[side * PLANES + zr] > 0.5
            dz = (zr - row_plane) & 7
            up, down = ways(dz, even)
            far[0] = jnp.maximum(far[0], jnp.where(wanted & up, dz, 0))
            far[1] = jnp.maximum(far[1], jnp.where(wanted & down, 8 - dz, 0))
        levels = jnp.concatenate(
            [jnp.where(far[way] == d, 1.0, 0.0) for way in range(2) for d in (4, 3, 2, 1)], axis=0
        )
        level_hot = levels.astype(BF16)
        before_lane = dot(level_hot, prefix, ((1,), (0,)))
        row_total = dot(level_hot, whole, ((1,), (0,))).astype(BF16)
        before_row = dot(rows_before, row_total, ((1,), (0,)))
        plane_total = dot(rows_all, row_total, ((1,), (0,)))
        for way in range(2):
            base = jnp.zeros((32, 256), F32)
            rank = jnp.zeros((32, 256), F32)
            for e in range(4):
                part = slice((way * 4 + e) * 32, (way * 4 + e) * 32 + 32)
                rank = rank + levels[part] * (base + before_row[part] + before_lane[part])
                base = base + plane_total[part]
                over = jnp.maximum(over, base - float(CAPS[3 - e]))
            if side == 0:
                ranks_all.append(rank.astype(jnp.int32) - 1)
                for p in range(PLANES):
                    rank_s[way, p] = ranks_all[way][p * 4 : p * 4 + 4]
    ok_ref[...] = jnp.broadcast_to(jnp.max(over, keepdims=True), (8, 128))

    plane = plane_ref[0]
    values = jnp.where(iota((8, 128), 0) == 0, iota((8, 128), 1), 1).astype(F32).astype(BF16)
    for way in range(2):
        mine = rank_s[way, plane]
        for g in range(GROUPS):
            index = jnp.zeros((1, LPAD), F32)
            for rr in range(4):
                ranks = mine[rr : rr + 1, g * 128 : g * 128 + 128]
                got = dot(values, hot(iota((LPAD, 128), 0) == ranks), ((1,), (1,)))
                index = index + got[0:1] + got[1:2] * float(rr * 128)
            lists_ref[way * GROUPS + g : way * GROUPS + g + 1, :] = index.astype(jnp.int32)

    dz = (plane - row_plane) & 7
    up, down = ways(dz, even)
    address = (iota((32, 256), 0) & 3) * 128 + (iota((32, 256), 1) & 127)
    for d in range(1, 5):
        address = jnp.where(up & (dz == d), ranks_all[0] + (OWN + OFFS[d - 1]), address)
        address = jnp.where(down & (8 - dz == d), ranks_all[1] + (OWN + CSUM + OFFS[d - 1]), address)
    digits = jnp.concatenate([address >> 5, address & 31], axis=1).astype(F32).astype(BF16)
    by_hi = hot(iota((32, 2048), 0) == hi_s[pl.ds(plane, 1), :])
    found = dot(digits, by_hi, ((0,), (0,)))
    at_code = iota((256, 2048), 0) == code_s[pl.ds(plane, 1), :]
    dest_hi = jnp.sum(jnp.where(at_code, found[:256], 0.0), axis=0, keepdims=True)
    dest_lo = jnp.sum(jnp.where(at_code, found[256:], 0.0), axis=0, keepdims=True)
    dest_ref[...] = (dest_hi * 32.0 + dest_lo).astype(jnp.int32)


def make_plan(block_ids, block_home, plane, tp_index):
    ids = block_ids.reshape(PLANES, SIDE, 2, HL, TOPK).transpose(2, 0, 1, 3, 4).reshape(2, PLANES, 2048)
    ids = jnp.where(tp_index == 0, ids, ids[::-1]).reshape(2 * PLANES, 2048)
    home = block_home.reshape(32, 32).T
    home = jnp.concatenate([home >> 5, home & 31], axis=0).astype(BF16)
    vmem = pl.BlockSpec(memory_space=pltpu.VMEM)
    return pl.pallas_call(
        plan_kernel,
        out_shape=(
            jax.ShapeDtypeStruct((4, LPAD), jnp.int32),
            jax.ShapeDtypeStruct((1, 2048), jnp.int32),
            jax.ShapeDtypeStruct((8, 128), F32),
        ),
        in_specs=[pl.BlockSpec(memory_space=pltpu.SMEM), vmem, vmem],
        out_specs=(vmem, vmem, vmem),
        scratch_shapes=[
            pltpu.VMEM((16, 32, 256), F32),
            pltpu.VMEM((16, 2048), jnp.int32),
            pltpu.VMEM((16, 2048), jnp.int32),
            pltpu.VMEM((2, PLANES, 4, 256), jnp.int32),
        ],
        compiler_params=pltpu.CompilerParams(vmem_limit_bytes=48 << 20),
        name="plan",
    )(plane.reshape(1), ids, home)


def pick(index, rows, width, base, data):
    def kernel(index_ref, data_ref, out_ref):
        for n, row in enumerate(rows):

            def one(j, carry):
                out_ref[0, n * width + j] = data_ref[0, index_ref[row, base + j]]
                return carry

            lax.fori_loop(0, width, one, 0, unroll=8)

    count = len(rows) * width
    return pl.pallas_call(
        kernel,
        grid=(2,),
        out_shape=jax.ShapeDtypeStruct((2, count, ROWS, HD), BF16),
        in_specs=[
            pl.BlockSpec(memory_space=pltpu.SMEM),
            pl.BlockSpec((1,) + data.shape[1:], lambda i: (i, 0, 0, 0)),
        ],
        out_specs=pl.BlockSpec((1, count, ROWS, HD), lambda i: (i, 0, 0, 0)),
        compiler_params=pltpu.CompilerParams(vmem_limit_bytes=48 << 20),
        name="pick",
    )(index, data)


def place():
    mem = lax.axis_index("mem")
    plane, me = mem // SIDE, mem % SIDE
    above = ((plane + 1) % PLANES) * SIDE + me
    below = ((plane + PLANES - 1) % PLANES) * SIDE + me
    return plane, me, lax.axis_index("tp"), (above, below)


def greet(ring):
    plane, me, tp, nexts = place()
    barrier = pltpu.get_barrier_semaphore()

    def one(k, carry):
        peer = plane * SIDE + (me + k) % SIDE
        pl.semaphore_signal(barrier, inc=1, device_id=(peer, tp), device_id_type=MESH)
        return carry

    lax.fori_loop(1, SIDE, one, 0)
    if ring:
        for peer in nexts:
            pl.semaphore_signal(barrier, inc=1, device_id=(peer, tp), device_id_type=MESH)
    pl.semaphore_wait(barrier, SIDE - 1 + (2 if ring else 0))


def spread(g, sources, own, send, recv):
    plane, me, tp, _ = place()
    for kv in range(2):

        def to_peer(k, carry):
            i = (me + k) % SIDE
            for h in range(HG):
                pltpu.make_async_remote_copy(
                    src_ref=sources[kv].at[:, i, :, pl.ds((g * HG + h) * HD, HD)],
                    dst_ref=own.at[kv, pl.ds(me * (HG * MB) + h * MB, MB)],
                    send_sem=send.at[kv],
                    recv_sem=recv.at[kv],
                    device_id=(plane * SIDE + i, tp),
                    device_id_type=MESH,
                ).start()
            return carry

        lax.fori_loop(1, SIDE, to_peer, 0)
        for h in range(HG):
            pltpu.make_async_copy(
                sources[kv].at[:, me, :, pl.ds((g * HG + h) * HD, HD)],
                own.at[kv, pl.ds(me * (HG * MB) + h * MB, MB)],
                recv.at[kv],
            ).start()


def spread_wait(own, send, recv):
    for kv in range(2):
        pltpu.make_async_copy(own.at[kv], own.at[kv], recv.at[kv]).wait()
        sent = own.at[kv, pl.ds(0, (SIDE - 1) * HG * MB)]
        pltpu.make_async_copy(sent, sent, send.at[kv]).wait()


def hop_copy(lst, pool, send, recv, kv, way, d):
    _, _, tp, nexts = place()
    count = CAPS[d]
    base = OWN + way * CSUM
    if d == 0:
        source = lst.at[kv, pl.ds(way * CAPS[0], count)]
    else:
        source = pool.at[kv, pl.ds(base + OFFS[d - 1], count)]
    return pltpu.make_async_remote_copy(
        src_ref=source,
        dst_ref=pool.at[kv, pl.ds(base + OFFS[d], count)],
        send_sem=send.at[kv, way, d],
        recv_sem=recv.at[kv, way, d],
        device_id=(nexts[way], tp),
        device_id_type=MESH,
    )


def hop(args, d):
    for kv in range(2):
        for way in range(2):
            if d > 0:
                hop_copy(*args, kv, way, d - 1).wait_recv()
            if d < 4:
                hop_copy(*args, kv, way, d).start()


def hops_sent(args):
    for kv in range(2):
        for way in range(2):
            for d in range(4):
                hop_copy(*args, kv, way, d).wait_send()


def deliver(given, rcv, send, recv):
    plane, me, tp, _ = place()
    for kv in range(2):

        def to_peer(k, carry):
            i = (me + k) % SIDE
            pltpu.make_async_remote_copy(
                src_ref=given.at[kv, pl.ds(i * SLOTS, SLOTS)],
                dst_ref=rcv.at[kv, me],
                send_sem=send.at[kv],
                recv_sem=recv.at[kv],
                device_id=(plane * SIDE + i, tp),
                device_id_type=MESH,
            ).start()
            return carry

        lax.fori_loop(1, SIDE, to_peer, 0)
        pltpu.make_async_copy(given.at[kv, pl.ds(me * SLOTS, SLOTS)], rcv.at[kv, me], recv.at[kv]).start()


def deliver_sent(given, send):
    for kv in range(2):
        sent = given.at[kv, pl.ds(0, (SIDE - 1) * SLOTS)]
        pltpu.make_async_copy(sent, sent, send.at[kv]).wait()


def softmax_dot(query, keys, visible):
    scores = dot(query, keys, ((1,), (1,)))
    if visible is not None:
        scores = jnp.where(visible, scores, -1e30)
    highest = jnp.max(scores, axis=1, keepdims=True)
    exponent = jnp.exp2((scores - highest) * SCALE)
    return (exponent * (1.0 / jnp.sum(exponent, axis=1, keepdims=True))).astype(BF16)


def columns(h):
    return pl.ds(pl.multiple_of(h * HD, HD), HD)


def attend_near(g, q_ref, k_ref, v_ref, near):
    def one(h, carry):
        cols = columns(g * HG + h)
        for rb in range(4):
            rows = pl.ds(rb * 128, 128)
            width = (rb + 1) * 128
            visible = iota((128, width), 0) + rb * 128 >= iota((128, width), 1)
            part = softmax_dot(q_ref[rows, cols], k_ref[pl.ds(0, width), cols], visible)
            near[rows, columns(h)] = dot(part, v_ref[pl.ds(0, width), cols], ((1,), (0,)))
        return carry

    lax.fori_loop(0, HG, one, 0)


def tile(rcv, kv, h):
    rows = rcv[kv, :, pl.ds(pl.multiple_of(h * TOPK, TOPK), TOPK)]
    return rows.astype(F32).reshape(SIDE * TOPK * ROWS, HD).astype(BF16)


def attend_keys(g, q_ref, rcv, recv, weights):
    pltpu.make_async_copy(rcv.at[0], rcv.at[0], recv.at[0]).wait()

    def one(h, carry):
        keys = tile(rcv, 0, h)
        cols = columns(g * HG + h)

        def block(rb, inner):
            rows = pl.ds(pl.multiple_of(rb * 128, 128), 128)
            weights[h, rows, :] = softmax_dot(q_ref[rows, cols], keys, None)
            return inner

        return lax.fori_loop(0, 4, block, carry)

    lax.fori_loop(0, HG, one, 0)


def attend_values(g, gate_ref, rcv, recv, weights, near, out_ref):
    pltpu.make_async_copy(rcv.at[1], rcv.at[1], recv.at[1]).wait()

    def one(h, carry):
        remote = dot(weights[h], tile(rcv, 1, h), ((1,), (0,)))
        gate = gate_ref[g * HG + h]
        out_ref[:, columns(h)] = (gate * remote + (1.0 - gate) * near[:, columns(h)]).astype(BF16)
        return carry

    lax.fori_loop(0, HG, one, 0)


def kernel_spread(mem_keys, mem_values, own, s1_send, s1_recv):
    greet(False)
    spread(0, (mem_keys, mem_values), own, s1_send, s1_recv)
    spread_wait(own, s1_send, s1_recv)


def kernel_ring(mem_keys, mem_values, own, lst, pool, own_next, *sems):
    s1_send, s1_recv, z_send, z_recv, copied = sems
    args = (lst, pool, z_send, z_recv)
    greet(True)
    hop(args, 0)
    spread(1, (mem_keys, mem_values), own_next, s1_send, s1_recv)
    keep = pltpu.make_async_copy(own, pool.at[:, pl.ds(0, OWN)], copied)
    keep.start()
    for d in range(1, 5):
        hop(args, d)
    spread_wait(own_next, s1_send, s1_recv)
    hops_sent(args)
    keep.wait()


def kernel_ring_attend(
    gate_ref, own, lst, given, q_ref, k_ref, v_ref, pool, out_ref, rcv, weights, near, *sems
):
    z_send, z_recv, s3_send, s3_recv, copied = sems
    args = (lst, pool, z_send, z_recv)
    greet(True)
    hop(args, 0)
    deliver(given, rcv, s3_send, s3_recv)
    keep = pltpu.make_async_copy(own, pool.at[:, pl.ds(0, OWN)], copied)
    keep.start()
    attend_near(0, q_ref, k_ref, v_ref, near)
    hop(args, 1)
    attend_keys(0, q_ref, rcv, s3_recv, weights)
    hop(args, 2)
    attend_values(0, gate_ref, rcv, s3_recv, weights, near, out_ref)
    hop(args, 3)
    hop(args, 4)
    hops_sent(args)
    deliver_sent(given, s3_send)
    keep.wait()


def kernel_attend(gate_ref, given, q_ref, k_ref, v_ref, out_ref, rcv, weights, near, s3_send, s3_recv):
    greet(False)
    deliver(given, rcv, s3_send, s3_recv)
    attend_near(1, q_ref, k_ref, v_ref, near)
    attend_keys(1, q_ref, rcv, s3_recv, weights)
    attend_values(1, gate_ref, rcv, s3_recv, weights, near, out_ref)
    deliver_sent(given, s3_send)


def fast_combined(lists, dest, gate, mem_keys, mem_values, queries, local_keys, local_values):
    smem = pl.BlockSpec(memory_space=pltpu.SMEM)
    hbm = pl.BlockSpec(memory_space=pl.ANY)
    vmem = pl.BlockSpec(memory_space=pltpu.VMEM)
    view = (MB, SIDE, ROWS, HL * HD)
    mem_keys, mem_values = mem_keys.reshape(view), mem_values.reshape(view)
    half = jax.ShapeDtypeStruct((queries.shape[0], HG * HD), BF16)
    own_shape = jax.ShapeDtypeStruct((2, OWN, ROWS, HD), BF16)
    pool_shape = jax.ShapeDtypeStruct((2, NPIECE, ROWS, HD), BF16)
    pair = pltpu.SemaphoreType.DMA((2,))
    ring = pltpu.SemaphoreType.DMA((2, 2, 4))
    one = pltpu.SemaphoreType.DMA
    attend_scratch = [
        pltpu.VMEM((2, SIDE, SLOTS, ROWS, HD), BF16),
        pltpu.VMEM((HG, 512, SIDE * TOPK * ROWS), BF16),
        pltpu.VMEM((512, HG * HD), F32),
    ]

    def call(kernel, name, number, outs, in_specs, out_specs, scratch, *args):
        return pl.pallas_call(
            kernel,
            out_shape=outs,
            in_specs=in_specs,
            out_specs=out_specs,
            scratch_shapes=scratch,
            compiler_params=pltpu.CompilerParams(
                collective_id=number, has_side_effects=True, vmem_limit_bytes=48 << 20
            ),
            name=name,
        )(*args)

    def far_lists(g, own):
        return pick(lists, (g, GROUPS + g), CAPS[0], 0, own)

    def requested(g, pool):
        return pick(dest, tuple(range(SIDE)), SLOTS, g * SLOTS, pool)

    own0 = call(
        kernel_spread, "spread", 0, own_shape, [hbm, hbm], hbm, [pair, pair], mem_keys, mem_values
    )
    lst0 = far_lists(0, own0)
    pool0, own1 = call(
        kernel_ring, "ring", 1, (pool_shape, own_shape), [hbm] * 4, (hbm, hbm),
        [pair, pair, ring, ring, one], mem_keys, mem_values, own0, lst0,
    )
    lst1 = far_lists(1, own1)
    given0 = requested(0, pool0)
    pool1, half0 = call(
        kernel_ring_attend, "ring_attend", 2, (pool_shape, half),
        [smem, hbm, hbm, hbm, vmem, vmem, vmem], (hbm, vmem),
        attend_scratch + [ring, ring, pair, pair, one],
        gate, own1, lst1, given0, queries, local_keys, local_values,
    )
    given1 = requested(1, pool1)
    half1 = call(
        kernel_attend, "attend", 3, half, [smem, hbm, vmem, vmem, vmem], vmem,
        attend_scratch + [pair, pair], gate, given1, queries, local_keys, local_values,
    )
    return half0, half1


def rank_within(owner_row):
    request_count = owner_row.shape[0]
    order_index = jnp.arange(request_count, dtype=jnp.int32)
    earlier = order_index[:, None] > order_index[None, :]
    same_owner = owner_row[:, None] == owner_row[None, :]
    return jnp.sum((same_owner & earlier).astype(jnp.int32), axis=1)


def slow_combined(gate, mem_keys, mem_values, queries, local_keys, local_values, block_ids, block_home):
    mem_count = lax.axis_size("mem")
    mem_index = lax.axis_index("mem")
    tp_index = lax.axis_index("tp")
    requests = HL * TOPK
    slots = 2
    group_ids = lax.dynamic_slice_in_dim(block_ids, tp_index * HL, HL, 1).reshape(mem_count, requests)
    home_slots = jnp.take(block_home, group_ids, axis=0)
    owners = home_slots // MB
    codes = (home_slots % MB) * HL + jnp.arange(requests, dtype=jnp.int32)[None, :] // TOPK
    own_owners = lax.dynamic_index_in_dim(owners, mem_index, 0, keepdims=False)
    own_codes = lax.dynamic_index_in_dim(codes, mem_index, 0, keepdims=False)
    own_ranks = rank_within(own_owners)
    slot_index = jnp.arange(slots, dtype=jnp.int32)
    owner_index = jnp.arange(mem_count, dtype=jnp.int32)
    matches = (own_owners[None, None, :] == owner_index[:, None, None]) & (
        own_ranks[None, None, :] == slot_index[None, :, None]
    )
    table = jnp.sum(jnp.where(matches, own_codes[None, None, :], 0), axis=2)
    wanted = lax.all_to_all(table, "mem", split_axis=0, concat_axis=0, tiled=True)
    flat_slot = own_owners * slots + own_ranks

    def fetch(rows):
        blocks = rows.reshape(MB, BLK, HL, HD)
        sent = blocks[wanted // HL, :, wanted % HL, :]
        got = lax.all_to_all(sent, "mem", split_axis=0, concat_axis=0, tiled=True)
        far = jnp.take(got.reshape(mem_count * slots, BLK, HD), flat_slot, axis=0)
        return far.reshape(HL, TOPK * BLK, HD)

    positions = jnp.arange(queries.shape[0], dtype=jnp.int32)
    causal = positions[:, None] >= positions[None, :]

    def by_head(x):
        return x.reshape(x.shape[0], HL, HD).transpose(1, 0, 2)

    def one_head(parts):
        q, far_k, far_v, near_k, near_v, g = parts
        remote = dot(softmax_dot(q, far_k, None), far_v, ((1,), (0,)))
        nearby = dot(softmax_dot(q, near_k, causal), near_v, ((1,), (0,)))
        return (g * remote + (1.0 - g) * nearby).astype(BF16)

    out = lax.map(
        one_head,
        (by_head(queries), fetch(mem_keys), fetch(mem_values), by_head(local_keys), by_head(local_values), gate),
    )
    out = out.reshape(GROUPS, HG, queries.shape[0], HD).transpose(0, 2, 1, 3)
    out = out.reshape(GROUPS, queries.shape[0], HG * HD)
    return out[0], out[1]


def per_device(
    queries, local_keys, local_values, mem_keys, mem_values, gate_bias, out_weight, block_ids, block_home
):
    mem_index = lax.axis_index("mem")
    tp_index = lax.axis_index("tp")
    gate = jax.nn.sigmoid(gate_bias)
    lists, dest, over = make_plan(block_ids, block_home, (mem_index // SIDE).astype(jnp.int32), tp_index)
    dest = dest.reshape(SIDE, HL * TOPK)
    half0, half1 = lax.cond(
        over[0, 0] <= 0.5,
        lambda: fast_combined(
            lists, dest, gate, mem_keys, mem_values, queries, local_keys, local_values
        ),
        lambda: slow_combined(
            gate, mem_keys, mem_values, queries, local_keys, local_values, block_ids, block_home
        ),
    )
    cut = HG * HD
    partial = jnp.dot(half0, out_weight[:cut], preferred_element_type=F32)
    partial = partial + jnp.dot(half1, out_weight[cut:], preferred_element_type=F32)
    mixed = lax.psum_scatter(partial, "tp", scatter_dimension=0, tiled=True)
    return mixed.astype(BF16)


def solution(mesh):
    in_specs = (
        P("mem", "tp"), P("mem", "tp"), P("mem", "tp"), P("mem", "tp"), P("mem", "tp"),
        P("tp"), P("tp", None), P(), P(),
    )
    return jax.shard_map(
        per_device, mesh=mesh, in_specs=in_specs, out_specs=P(("mem", "tp"), None), check_vma=False
    )
```

time: 578 us -> 366 us (0.63); the launches traced: 571 us -> 366 us
  waiting for transfers between devices: 351 us -> 33.9 us
  Pallas kernels: 0 us -> 296 us
  local copies, waits for them, and re-layouts: 111 us -> 11.1 us
  starting transfers between devices: 37.5 us -> 0.04 us
  matrix products: 36.8 us -> 6.33 us
  other arithmetic: 15.1 us -> 3.58 us
    all_to_all x3 -> x0, waiting for transfers between devices: 331 us -> none  [the longest x1 170 us: per_device(): lax.all_to_all(sent_keys, 'mem', split_axis=0, concat_axis=0, tiled=True)]
    pallas_call x0 -> x9, Pallas kernels: none -> 296 us  [the longest x4 257 us: call(): pl.pallas_call(kernel, out_shape=outs, in_specs=in_specs, out_specs=out_s...]
    gather x6 -> x0, local copies, waits for them, and re-layouts: 97.8 us -> none  [the longest x2 65.4 us: per_device(): home_slots = jnp.take(block_home, group_ids, axis=0)]
    all_to_all x3 -> x0, starting transfers between devices: 37.5 us -> none  [the longest x1 16.3 us: per_device(): lax.all_to_all(table, 'mem', split_axis=0, concat_axis=0, tiled=True)]
    dot_general x33 -> x2, matrix products: 36.8 us -> 6.33 us  [the longest x1 3.3 us: per_device(): jnp.dot(half1, out_weight[cut:], preferred_element_type=F32)]
    reduce_scatter x1, waiting for transfers between devices: 19.8 us -> 33.9 us  [per_device(): mixed = lax.psum_scatter(partial, 'tp', scatter_dimension=0, tiled=True)]
    unnamed x40 -> x12, local copies, waits for them, and re-layouts: 9.19 us -> 0.03 us
    reduce_sum x18 -> x0, other arithmetic: 7.93 us -> none  [the longest x16 7.64 us: attend(): jnp.sum(exponent, axis=1, keepdims=True)]
  transfers between devices with their start and end apart: 4 -> 1, of which waited for: 4 -> 1; matrix products, arithmetic and copies ran while one was open for 6% -> 0% of each run, Pallas kernels for 0% -> 0%
where the time goes in v1:
time: 366 us
  Pallas kernels  296 us (81%)
  waiting for transfers between devices  33.9 us (9%)
  between operations  14.2 us (4%)
  local copies, waits for them, and re-layouts  11.1 us (3%)
  matrix products  6.33 us (2%)
    pallas_call x4, Pallas kernels, call(): pl.pallas_call(kernel, out_shape=outs, in_specs=in_specs, out_specs=out_s...  257 us
    reduce_scatter x1, waiting for transfers between devices, per_device(): mixed = lax.psum_scatter(partial, 'tp', scatter_dimension=0, tiled=True)  33.9 us
    pallas_call x4, Pallas kernels, pick(): pl.pallas_call(kernel, grid=(2,), out_shape=jax.ShapeDtypeStruct((2, coun...  26.8 us
    pallas_call x1, Pallas kernels, make_plan(): pl.pallas_call(plan_kernel, out_shape=(jax.ShapeDtypeStruct((4, LPAD), jn...  12.2 us
  transfers between devices with their start and end apart: 1, of which 1 were waited for; matrix products, arithmetic and copies ran while one was open for 0% of the time, Pallas kernels for 0%

profile of v1, /device:TPU:1, one launch (start us, length us, event | category | flops | bytes accessed | tf_op | source)
XLA Modules:
  0.0 365.5 jit_solution(18000278178431108168)
XLA Ops:
  6.5 0.0 copy-start.2
  6.5 0.0 copy-start.13
  6.5 0.0 copy-start.14
  6.5 0.0 copy-start.6
  6.5 0.0 copy-start.3
  6.5 0.0 reduce-scatter.2.cloned.1.call-start
  6.6 0.8 shift-right-arithmetic_convert_fusion
  7.4 0.1 shift_right_arithmetic.14
  7.5 0.1 copy.67
  7.6 0.1 and.113
  7.7 0.1 copy.68
  7.8 2.2 reshape.336
  10.0 2.6 copy.66
  12.6 1.8 reshape.337
  14.4 0.0 copy-done.14
  14.5 12.2 %plan.1 = (s32[4,384]{1,0:T(4,128)S(1)}, s32[1,2048]{1,0:T(1,128)S(1)}, f32[8,128]{1,0:T(8,128)S(1)}) custom-call(s32[1]{0:T(128)} %bitcast.23.plane_ref, s32[16,2048]{1,0:T(8,128)S(1)} %fusion.45.ids_ref, bf16[64,32]{1,0:T(8,128)(2,1)S(1)} %pad_maximum_fusion.home_ref), custom_call_target="tpu_custom_call" | custom-call | tf_op jit(solution)/shard_map/plan/pallas_call | solution.py:149
  26.7 0.5 slice.17
  27.9 0.0 copy-done.2
  27.9 0.0 copy-done.13
  27.9 0.0 copy-done.6
  27.9 0.0 copy-done.3
  27.9 287.8 %conditional.1 = (bf16[512,512]{1,0:T(8,128)(2,1)S(1)}, bf16[512,512]{1,0:T(8,128)(2,1)S(1)}) conditional(s32[]{:T(128)} %bitcast.28, (bf16[512,1024]{1,0:T(8,128)(2,1)S(1)}, bf16[1024,1024]{1,0:T(8,128)(2,1)S(1)}, s32[128,16,16]{0,2,1:T(8,128)S(1)}, s32[1024]{0:T(1024)S(1)}, bf16[1024,1024]{1,0:T(8,128)(2,1)}, ...), branch_computations={%region_0.10_spmd, %region_9.11_spmd} | conditional | flops 687058048 | bytes 187169344 | solution.py:551
  28.1 0.0 copy-start.5
  28.2 34.5 %spread.1.data_ref.own = bf16[2,512,8,128]{3,2,1,0:T(8,128)(2,1)S(1)} custom-call(bf16[8,16,8,1024]{3,2,1,0:T(8,128)(2,1)S(1)} %bitcast.129, bf16[8,16,8,1024]{3,2,1,0:T(8,128)(2,1)} %bitcast.132), custom_call_target="tpu_custom_call" | custom-call | tf_op jit(solution)/shard_map/cond/branch_1_fun/spread/pallas_call | solution.py:443
  62.6 4.5 %pick.4.lst = bf16[2,688,8,128]{3,2,1,0:T(8,128)(2,1)S(1)} custom-call(s32[4,384]{1,0:T(4,128)S(1)} %get-tuple-element.186.index_ref, bf16[2,512,8,128]{3,2,1,0:T(8,128)(2,1)S(1)} %spread.1.data_ref.own), custom_call_target="tpu_custom_call" | custom-call | tf_op jit(solution)/shard_map/cond/branch_1_fun/pick/pallas_call | solution.py:180
  67.2 0.0 copy-start.1
  67.2 1.5 copy-done.1
  68.7 0.0 copy-done.5
  68.7 86.7 %ring.1 = (bf16[2,2336,8,128]{3,2,1,0:T(8,128)(2,1)}, bf16[2,512,8,128]{3,2,1,0:T(8,128)(2,1)S(1)}) custom-call(bf16[8,16,8,1024]{3,2,1,0:T(8,128)(2,1)S(1)} %bitcast.130, bf16[8,16,8,1024]{3,2,1,0:T(8,128)(2,1)S(1)} %bitcast.133, bf16[2,512,8,128]{3,2,1,0:T(8,128)(2,1)S(1)} %spread.1.data_ref.own, bf16[2,688,8,128]{3,2,1,0:T(8,128)(2,1)} %copy-done.1), custom_call_target="tpu_custom_call" | custom-call | tf_op jit(solution)/shard_map/cond/branch_1_fun/ring/pallas_call | solution.py:443
  155.4 4.7 %pick.5.lst = bf16[2,688,8,128]{3,2,1,0:T(8,128)(2,1)S(1)} custom-call(s32[4,384]{1,0:T(4,128)S(1)} %get-tuple-element.186.index_ref, bf16[2,512,8,128]{3,2,1,0:T(8,128)(2,1)S(1)} %get-tuple-element.187.data_ref.own), custom_call_target="tpu_custom_call" | custom-call | tf_op jit(solution)/shard_map/cond/branch_1_fun/pick/pallas_call | solution.py:180
  160.1 0.0 copy-start.8
  160.1 0.0 copy-start.10
  160.1 8.6 %pick.6.given = bf16[2,1024,8,128]{3,2,1,0:T(8,128)(2,1)S(1)} custom-call(s32[16,128]{1,0:T(8,128)S(1)} %bitcast.147, bf16[2,2336,8,128]{3,2,1,0:T(8,128)(2,1)} %get-tuple-element.189.data_ref), custom_call_target="tpu_custom_call" | custom-call | tf_op jit(solution)/shard_map/cond/branch_1_fun/pick/pallas_call | solution.py:180
  168.8 0.0 copy-start
  168.8 2.1 copy-done
  170.9 0.0 copy-done.8
  170.9 0.0 copy-done.10
  170.9 85.5 %ring_attend.1 = (bf16[2,2336,8,128]{3,2,1,0:T(8,128)(2,1)}, bf16[512,512]{1,0:T(8,128)(2,1)S(1)}) custom-call(f32[8]{0:T(128)S(1)} %get-tuple-element.183.gate_ref, bf16[2,512,8,128]{3,2,1,0:T(8,128)(2,1)S(1)} %get-tuple-element.187.data_ref.own, bf16[2,688,8,128]{3,2,1,0:T(8,128)(2,1)S(1)} %pick.5.lst, bf16[2,1024,8,128]{3,2,1,0:T(8,128)(2,1)} %copy-done, ...), custom_call_target="tpu_custom_call" | custom-call | tf_op jit(solution)/shard_map/cond/branch_1_fun/ring_attend/pallas_call | solution.py:443
  256.3 9.0 %pick.7.given = bf16[2,1024,8,128]{3,2,1,0:T(8,128)(2,1)S(1)} custom-call(s32[16,128]{1,0:T(8,128)S(1)} %bitcast.148, bf16[2,2336,8,128]{3,2,1,0:T(8,128)(2,1)} %get-tuple-element.194.data_ref), custom_call_target="tpu_custom_call" | custom-call | tf_op jit(solution)/shard_map/cond/branch_1_fun/pick/pallas_call | solution.py:180
  265.3 50.4 %attend.1 = bf16[512,512]{1,0:T(8,128)(2,1)S(1)} custom-call(f32[8]{0:T(128)S(1)} %get-tuple-element.183.gate_ref, bf16[2,1024,8,128]{3,2,1,0:T(8,128)(2,1)S(1)} %pick.7.given, bf16[512,1024]{1,0:T(8,128)(2,1)S(1)} %get-tuple-element.190.q_ref, bf16[512,1024]{1,0:T(8,128)(2,1)S(1)} %copy-done.8, bf16[512,1024]{1,0:T(8,128)(2,1)S(1)} %copy-done.10), custom_call_target="tpu_custom_call" | custom-call | tf_op jit(solution)/shard_map/cond/branch_1_fun/attend/pallas_call | solution.py:443
  315.7 0.0 copy-start.11
  315.7 3.0 fusion.43
  318.8 0.0 copy-done.11
  318.8 3.3 convolution_add_fusion
  322.1 0.0 reduce-scatter.2.cloned.1.call-update
  322.1 33.9 %reduce-scatter.2.cloned.1.call-done = f32[256,2048]{1,0:T(8,128)} async-done(((f32[512,2048]{1,0:T(8,128)}), f32[256,2048]{1,0:T(8,128)}) %reduce-scatter.2.cloned.1.call-update) | async-done | bytes 2097168 | tf_op jit(solution)/shard_map/reduce_scatter | solution.py:563
  356.0 2.7 convert_element_type.36
  (3 shorter events, 0.0 us)
Async XLA Ops:
  6.5 21.3 %copy-start.2 = (s32[1024]{0:T(1024)S(1)}, s32[1024]{0:T(1024)}, u32[]{:S(2)}) copy-start(s32[1024]{0:T(1024)} %param.23) | copy-start | bytes 12292
  6.5 21.3 %copy-start.13 = (s32[128,16,16]{0,2,1:T(8,128)S(1)}, s32[128,16,16]{0,2,1:T(8,128)}, u32[]{:S(2)}) copy-start(s32[128,16,16]{0,2,1:T(8,128)} %param.22) | copy-start | bytes 393220
  6.5 7.9 %copy-start.14 = (f32[8]{0:T(128)S(1)}, f32[8]{0:T(128)}, u32[]{:S(2)}) copy-start(f32[8]{0:T(128)} %param.20) | copy-start | bytes 100
  6.5 21.3 %copy-start.6 = (bf16[512,1024]{1,0:T(8,128)(2,1)S(1)}, bf16[512,1024]{1,0:T(8,128)(2,1)}, u32[]{:S(2)}) copy-start(bf16[512,1024]{1,0:T(8,128)(2,1)} %param.15) | copy-start | bytes 3145732
  6.5 21.4 %copy-start.3 = (bf16[1024,1024]{1,0:T(8,128)(2,1)S(1)}, bf16[1024,1024]{1,0:T(8,128)(2,1)}, u32[]{:S(2)}) copy-start(bf16[1024,1024]{1,0:T(8,128)(2,1)} %param.18) | copy-start | bytes 6291460
  6.5 349.4 %reduce-scatter.2.cloned.1.call-start = ((), (), s32[]{:S(2)}) async-start(), calls=%async_computation.4 | async-start | bytes 6291456 | tf_op jit(solution)/shard_map/reduce_scatter | solution.py:563
  28.1 40.6 %copy-start.5 = (bf16[1024,1024]{1,0:T(8,128)(2,1)S(1)}, bf16[1024,1024]{1,0:T(8,128)(2,1)}, u32[]{:S(2)}) copy-start(bf16[1024,1024]{1,0:T(8,128)(2,1)} %get-tuple-element.185) | copy-start | bytes 6291460 | tf_op jit(solution)/shard_map/cond
  67.2 1.5 copy-start.1
  160.1 10.7 %copy-start.8 = (bf16[512,1024]{1,0:T(8,128)(2,1)S(1)}, bf16[512,1024]{1,0:T(8,128)(2,1)}, u32[]{:S(2)}) copy-start(bf16[512,1024]{1,0:T(8,128)(2,1)} %get-tuple-element.191.k_ref) | copy-start | bytes 3145732 | tf_op jit(solution)/shard_map/cond
  160.1 10.7 %copy-start.10 = (bf16[512,1024]{1,0:T(8,128)(2,1)S(1)}, bf16[512,1024]{1,0:T(8,128)(2,1)}, u32[]{:S(2)}) copy-start(bf16[512,1024]{1,0:T(8,128)(2,1)} %get-tuple-element.192.v_ref) | copy-start | bytes 3145732 | tf_op jit(solution)/shard_map/cond
  168.8 2.1 copy-start
  315.7 3.1 copy-start.11
Sparse Core Ops, SparseCore 0:
  322.2 33.7 reduce-scatter.1

commit v2 on v0

v2 whole, which is shorter than its diff:
```python
import functools
import math

import jax
import jax.numpy as jnp
from jax import lax
from jax.experimental import pallas as pl
from jax.experimental.pallas import tpu as pltpu
from jax.sharding import PartitionSpec as P

HD = 128
BLK = 128
TOPK = 16
PLANES = 8
SIDE = 16
HL = 8
GROUPS = 2
HG = HL // GROUPS
MB = 8
ROWS = BLK // SIDE
OWN = SIDE * MB * HG
CAPS = (344, 280, 200, 88)
OFFS = (0, 344, 624, 824)
CSUM = 912
CUTS = (0, 88, 200, 280, 344)
NPIECE = OWN + 2 * CSUM
PIECE = 2 * ROWS
LPAD = 384
SLOTS = HG * TOPK
MESH = pl.DeviceIdType.MESH
F32 = jnp.float32
BF16 = jnp.bfloat16
SCALE = math.log2(math.e) / math.sqrt(HD)


def iota(shape, axis):
    return lax.broadcasted_iota(jnp.int32, shape, axis)


def hot(mask):
    return jnp.where(mask, 1.0, 0.0).astype(BF16)


def dot(a, b, dims):
    return lax.dot_general(a, b, (dims, ((), ())), preferred_element_type=F32)


def ways(dz, even):
    up = ((dz >= 1) & (dz <= 3)) | ((dz == 4) & even)
    down = (dz >= 5) | ((dz == 4) & jnp.logical_not(even))
    return up, down


def plan(ids_ref, home_ref, lists_ref, dest_ref, over_ref, rank_s, address_s, plane, tp):
    home = home_ref[...]
    home = jnp.concatenate([home >> 5, home & 31], axis=0).astype(F32).astype(BF16)
    lane = iota((1, 2048), 1)
    plane_term = ((lane & 127) >> 4) * 32
    row_plane = iota((32, 256), 0) >> 2
    even = (iota((32, 256), 1) & 1) == 0
    dz = ((iota((32, 256), 1) >> 5) - row_plane) & 7
    up, down = ways(dz, even)
    reach = (jnp.where(up, dz, 0), jnp.where(down, 8 - dz, 0))

    def find(side, h):
        block = ids_ref[side, h]
        ids = jnp.concatenate([block[q : q + 1] for q in range(TOPK)], axis=1)
        both = dot(home, hot(iota((128, 2048), 0) == (ids & 127)), ((1,), (0,)))
        at_hi = iota((8, 2048), 0) == (ids >> 7)
        pos_hi = jnp.sum(jnp.where(at_hi, both[:8], 0.0), axis=0, keepdims=True).astype(jnp.int32)
        pos_lo = jnp.sum(jnp.where(at_hi, both[8:], 0.0), axis=0, keepdims=True).astype(jnp.int32)
        return hot(iota((32, 2048), 0) == pos_hi), pos_lo

    r, s = iota((256, 256), 0), iota((256, 256), 1)
    same_group = (r >> 7) == (s >> 7)
    prefix = hot(same_group & (r <= s))
    whole = hot(same_group)
    same_plane = (r >> 2) == (s >> 2)
    rows_before = hot(same_plane & (s < r))
    rows_all = hot(same_plane)
    over = jnp.zeros((32, 256), F32)
    ranks = []
    for other in range(2):
        side = tp if other == 0 else 1 - tp

        def one_head(h, far):
            by_hi, pos_lo = find(side, h)
            count = dot(by_hi, hot(iota((256, 2048), 0) == plane_term + pos_lo), ((1,), (1,)))
            out = []
            for way in range(2):
                value = jnp.where(count > 0.5, reach[way], 0)
                for shift in (128, 64, 32):
                    value = jnp.maximum(value, pltpu.roll(value, shift, 1))
                out.append(jnp.where((iota((32, 256), 1) >> 5) == h, value, far[way]))
            return tuple(out)

        zero = jnp.zeros((32, 256), jnp.int32)
        far = lax.fori_loop(0, HL, one_head, (zero, zero))
        levels = jnp.concatenate(
            [jnp.where(far[way] == d, 1.0, 0.0) for way in range(2) for d in (4, 3, 2, 1)], axis=0
        )
        level_hot = levels.astype(BF16)
        before_lane = dot(level_hot, prefix, ((1,), (0,)))
        row_total = dot(level_hot, whole, ((1,), (0,))).astype(BF16)
        before_row = dot(rows_before, row_total, ((1,), (0,)))
        plane_total = dot(rows_all, row_total, ((1,), (0,)))
        for way in range(2):
            base = jnp.zeros((32, 256), F32)
            rank = jnp.zeros((32, 256), F32)
            for e in range(4):
                part = slice((way * 4 + e) * 32, (way * 4 + e) * 32 + 32)
                rank = rank + levels[part] * (base + before_row[part] + before_lane[part])
                base = base + plane_total[part]
                over = jnp.maximum(over, base - float(CAPS[3 - e]))
            if other == 0:
                ranks.append(rank.astype(jnp.int32) - 1)
                for p in range(PLANES):
                    rank_s[way, p] = ranks[way][p * 4 : p * 4 + 4]
    over_ref[...] = jnp.broadcast_to(jnp.max(over, keepdims=True), (8, 128))

    values = jnp.where(iota((8, 128), 0) == 0, iota((8, 128), 1), 1).astype(F32).astype(BF16)
    for way in range(2):
        mine = rank_s[way, plane]
        for g in range(GROUPS):
            index = jnp.zeros((1, LPAD), F32)
            for rr in range(4):
                wanted = mine[rr : rr + 1, g * 128 : g * 128 + 128]
                got = dot(values, hot(iota((LPAD, 128), 0) == wanted), ((1,), (1,)))
                index = index + got[0:1] + got[1:2] * float(rr * 128)
            lists_ref[g * 2 + way : g * 2 + way + 1, :] = index.astype(jnp.int32)

    dz = (plane - row_plane) & 7
    up, down = ways(dz, even)
    address = (iota((32, 256), 0) & 3) * 128 + (iota((32, 256), 1) & 127)
    for d in range(1, 5):
        address = jnp.where(up & (dz == d), ranks[0] + (OWN + OFFS[d - 1]), address)
        address = jnp.where(down & (8 - dz == d), ranks[1] + (OWN + CSUM + OFFS[d - 1]), address)
    high = jnp.transpose((address >> 5).astype(F32))
    low = jnp.transpose((address & 31).astype(F32))
    for h in range(HL):
        part = slice(h * 32, h * 32 + 32)
        address_s[h] = jnp.concatenate([high[part], low[part]], axis=0)

    def one_dest(h, carry):
        by_hi, pos_lo = find(tp, h)
        found = dot(address_s[h].astype(BF16), by_hi, ((1,), (0,)))
        at_lo = iota((32, 2048), 0) == pos_lo
        dest_hi = jnp.sum(jnp.where(at_lo, found[:32], 0.0), axis=0, keepdims=True)
        dest_lo = jnp.sum(jnp.where(at_lo, found[32:], 0.0), axis=0, keepdims=True)
        dest = (dest_hi * 32.0 + dest_lo).astype(jnp.int32)
        rows = jnp.concatenate([dest[:, q * 128 : q * 128 + 128] for q in range(TOPK)], axis=0)
        dest_ref[pl.ds(pl.multiple_of(h * TOPK, TOPK), TOPK), :] = rows
        return carry

    lax.fori_loop(0, HL, one_dest, 0)


def pick_list(g, lists_ref, own, out):
    for way in range(2):

        def one(j, carry):
            out[way * CAPS[0] + j] = own[lists_ref[g * 2 + way, j]]
            return carry

        lax.fori_loop(0, CAPS[0], one, 0, unroll=8)


def pick_requests(g, r, dest_ref, pool, out):
    column = (lax.axis_index("mem") // SIDE) * SIDE + r

    def one(j, carry):
        out[r * SLOTS + j] = pool[dest_ref[g * SLOTS + j, column]]
        return carry

    lax.fori_loop(0, SLOTS, one, 0, unroll=16)


def pick(name, list_group, request_group, lists, dest, own_next, own, ring):
    smem = pl.BlockSpec(memory_space=pltpu.SMEM)
    hbm = pl.BlockSpec(memory_space=pl.ANY)
    with_list, with_requests = own_next is not None, own is not None
    steps = 4

    def kernel(*refs):
        refs = list(refs)
        lists_ref, dest_ref = refs.pop(0), refs.pop(0)
        next_hbm = refs.pop(0) if with_list else None
        own_hbm, ring_hbm = (refs.pop(0), refs.pop(0)) if with_requests else (None, None)
        list_hbm = refs.pop(0) if with_list else None
        given_hbm = refs.pop(0) if with_requests else None
        in_sem, out_sem = refs.pop(), refs.pop()
        if with_list:
            next_v, list_v = refs.pop(0), refs.pop(0)
            next_in = pltpu.make_async_copy(next_hbm, next_v, in_sem.at[0])
            next_in.start()
        if with_requests:
            pool_v, given_v = refs.pop(0), refs.pop(0)
            own_in = pltpu.make_async_copy(own_hbm, pool_v.at[pl.ds(0, OWN)], in_sem.at[1])
            ring_in = pltpu.make_async_copy(ring_hbm, pool_v.at[pl.ds(OWN, 2 * CSUM)], in_sem.at[2])
            own_in.start()
            ring_in.start()
        outs = []
        if with_list:
            next_in.wait()
            pick_list(list_group, lists_ref, next_v, list_v)
            outs.append(pltpu.make_async_copy(list_v, list_hbm, out_sem.at[steps]))
            outs[-1].start()
        if with_requests:
            own_in.wait()
            ring_in.wait()
            for step in range(steps):
                wide = SIDE // steps

                def one(r, carry):
                    pick_requests(request_group, r, dest_ref, pool_v, given_v)
                    return carry

                lax.fori_loop(step * wide, step * wide + wide, one, 0)
                part = pl.ds(step * wide * SLOTS, wide * SLOTS)
                outs.append(pltpu.make_async_copy(given_v.at[part], given_hbm.at[part], out_sem.at[step]))
                outs[-1].start()
        for out in outs:
            out.wait()

    def piece(count):
        return (count, PIECE, HD)

    shapes, scratch, data = [], [], []
    if with_list:
        shapes.append(jax.ShapeDtypeStruct(piece(2 * CAPS[0]), BF16))
        scratch += [pltpu.VMEM(piece(OWN), BF16), pltpu.VMEM(piece(2 * CAPS[0]), BF16)]
        data.append(own_next)
    if with_requests:
        shapes.append(jax.ShapeDtypeStruct(piece(SIDE * SLOTS), BF16))
        scratch += [pltpu.VMEM(piece(NPIECE), BF16), pltpu.VMEM(piece(SIDE * SLOTS), BF16)]
        data += [own, ring]
    return pl.pallas_call(
        kernel,
        out_shape=tuple(shapes),
        in_specs=[smem, smem] + [hbm] * len(data),
        out_specs=tuple([hbm] * len(shapes)),
        scratch_shapes=scratch + [pltpu.SemaphoreType.DMA((steps + 1,)), pltpu.SemaphoreType.DMA((3,))],
        compiler_params=pltpu.CompilerParams(vmem_limit_bytes=48 << 20),
        name=name,
    )(lists, dest, *data)


def place():
    mem = lax.axis_index("mem")
    plane, me = mem // SIDE, mem % SIDE
    above = ((plane + 1) % PLANES) * SIDE + me
    below = ((plane + PLANES - 1) % PLANES) * SIDE + me
    return plane, me, lax.axis_index("tp"), (above, below)


def greet(ring, partner):
    plane, me, tp, nexts = place()
    barrier = pltpu.get_barrier_semaphore()

    def one(k, carry):
        peer = plane * SIDE + (me + k) % SIDE
        pl.semaphore_signal(barrier, inc=1, device_id=(peer, tp), device_id_type=MESH)
        return carry

    lax.fori_loop(1, SIDE, one, 0)
    count = SIDE - 1
    if ring:
        for peer in nexts:
            pl.semaphore_signal(barrier, inc=1, device_id=(peer, tp), device_id_type=MESH)
        count += 2
    if partner:
        pl.semaphore_signal(
            barrier, inc=1, device_id=(plane * SIDE + me, 1 - tp), device_id_type=MESH
        )
        count += 1
    pl.semaphore_wait(barrier, count)


def spread(g, sources, own, send, recv):
    plane, me, tp, _ = place()
    base = (me // 4) * 128 + (me % 4) * MB

    def parts(i):
        for h in range(HG):
            for kv in range(2):
                yield (
                    sources[kv].at[:, i, :, pl.ds((g * HG + h) * HD, HD)],
                    own.at[pl.ds(base + h * 32, MB), pl.ds(kv * ROWS, ROWS)],
                )

    def to_peer(k, carry):
        i = (me + k) % SIDE
        for source, target in parts(i):
            pltpu.make_async_remote_copy(
                src_ref=source,
                dst_ref=target,
                send_sem=send,
                recv_sem=recv,
                device_id=(plane * SIDE + i, tp),
                device_id_type=MESH,
            ).start()
        return carry

    lax.fori_loop(1, SIDE, to_peer, 0)
    for source, target in parts(me):
        pltpu.make_async_copy(source, target, recv).start()


def spread_wait(own, send, recv):
    pltpu.make_async_copy(own, own, recv).wait()
    sent = own.at[pl.ds(0, (SIDE - 1) * HG * MB)]
    pltpu.make_async_copy(sent, sent, send).wait()


def hop_copy(lst, ring, send, recv, way, part, d):
    _, _, tp, nexts = place()
    low, count = CUTS[part], CUTS[part + 1] - CUTS[part]
    base = way * CSUM + low
    if d == 0:
        source = lst.at[pl.ds(way * CAPS[0] + low, count)]
    else:
        source = ring.at[pl.ds(base + OFFS[d - 1], count)]
    return pltpu.make_async_remote_copy(
        src_ref=source,
        dst_ref=ring.at[pl.ds(base + OFFS[d], count)],
        send_sem=send.at[way, part, d],
        recv_sem=recv.at[way, part, d],
        device_id=(nexts[way], tp),
        device_id_type=MESH,
    )


def hop_first(args):
    for part in range(4):
        for way in range(2):
            hop_copy(*args, way, part, 0).start()


def hop_on(args, d):
    for part in range(4 - d):
        for way in range(2):
            hop_copy(*args, way, part, d - 1).wait_recv()
            hop_copy(*args, way, part, d).start()


def hop_last(args):
    for part in range(4):
        for way in range(2):
            hop_copy(*args, way, part, 3 - part).wait_recv()
            for d in range(4 - part):
                hop_copy(*args, way, part, d).wait_send()


def deliver(given, rcv, send, recv):
    plane, me, tp, _ = place()
    for h in range(HG):

        def to_peer(k, carry):
            i = (me + k) % SIDE
            pltpu.make_async_remote_copy(
                src_ref=given.at[pl.ds(i * SLOTS + h * TOPK, TOPK)],
                dst_ref=rcv.at[h, me],
                send_sem=send,
                recv_sem=recv.at[h],
                device_id=(plane * SIDE + i, tp),
                device_id_type=MESH,
            ).start()
            return carry

        lax.fori_loop(1, SIDE, to_peer, 0)
        pltpu.make_async_copy(
            given.at[pl.ds(me * SLOTS + h * TOPK, TOPK)], rcv.at[h, me], recv.at[h]
        ).start()


def deliver_sent(given, send):
    sent = given.at[pl.ds(0, (SIDE - 1) * SLOTS)]
    pltpu.make_async_copy(sent, sent, send).wait()


def softmax_dot(query, keys, visible):
    scores = dot(query, keys, ((1,), (1,)))
    if visible is not None:
        scores = jnp.where(visible, scores, -1e30)
    highest = jnp.max(scores, axis=1, keepdims=True)
    exponent = jnp.exp2((scores - highest) * SCALE)
    return (exponent * (1.0 / jnp.sum(exponent, axis=1, keepdims=True))).astype(BF16)


def columns(h):
    return pl.ds(pl.multiple_of(h * HD, HD), HD)


def attend_near(g, q_ref, k_ref, v_ref, near):
    def one(h, carry):
        cols = columns(g * HG + h)
        for rb in range(4):
            rows = pl.ds(rb * 128, 128)
            width = (rb + 1) * 128
            visible = iota((128, width), 0) + rb * 128 >= iota((128, width), 1)
            part = softmax_dot(q_ref[rows, cols], k_ref[pl.ds(0, width), cols], visible)
            near[rows, columns(h)] = dot(part, v_ref[pl.ds(0, width), cols], ((1,), (0,)))
        return carry

    lax.fori_loop(0, HG, one, 0)


def attend_far(g, low, high, gate_ref, q_ref, rcv, recv, near, out_ref, done):
    def one(h, carry):
        pltpu.make_async_copy(rcv.at[h], rcv.at[h], recv.at[h]).wait()
        rows = rcv[h].astype(F32).reshape(SIDE * TOPK, PIECE, HD)
        keys = rows[:, :ROWS].reshape(SIDE * TOPK * ROWS, HD).astype(BF16)
        values = rows[:, ROWS:].reshape(SIDE * TOPK * ROWS, HD).astype(BF16)
        cols = columns(g * HG + h)
        gate = gate_ref[g * HG + h]

        def block(rb, inner):
            rows = pl.ds(pl.multiple_of(rb * 128, 128), 128)
            remote = dot(softmax_dot(q_ref[rows, cols], keys, None), values, ((1,), (0,)))
            mixed = gate * remote + (1.0 - gate) * near[rows, columns(h)]
            out_ref[rows, columns(h)] = mixed.astype(BF16)
            return inner

        lax.fori_loop(0, 4, block, 0)
        if done is not None:
            done(h)
        return carry

    lax.fori_loop(low, high, one, 0)


def kernel_spread(
    mem_keys, mem_values, ids_ref, home_ref, own, lists_ref, dest_ref, over_ref, rank_s, address_s, send, recv
):
    plane, _, tp, _ = place()
    greet(False, False)
    spread(0, (mem_keys, mem_values), own, send, recv)
    plan(ids_ref, home_ref, lists_ref, dest_ref, over_ref, rank_s, address_s, plane, tp)
    spread_wait(own, send, recv)


def kernel_ring(mem_keys, mem_values, weight, lst, ring, own_next, other_weight, *sems):
    s1_send, s1_recv, z_send, z_recv, w_sems = sems
    plane, me, tp, _ = place()
    args = (lst, ring, z_send, z_recv)
    greet(True, True)
    hop_first(args)
    spread(1, (mem_keys, mem_values), own_next, s1_send, s1_recv)
    swap = pltpu.make_async_remote_copy(
        src_ref=weight,
        dst_ref=other_weight,
        send_sem=w_sems.at[0],
        recv_sem=w_sems.at[1],
        device_id=(plane * SIDE + me, 1 - tp),
        device_id_type=MESH,
    )
    swap.start()
    for d in range(1, 4):
        hop_on(args, d)
    hop_last(args)
    spread_wait(own_next, s1_send, s1_recv)
    swap.wait()


def kernel_ring_attend(gate_ref, lst, given, q_ref, k_ref, v_ref, ring, out_ref, rcv, near, *sems):
    z_send, z_recv, s3_send, s3_recv = sems
    args = (lst, ring, z_send, z_recv)
    far = (gate_ref, q_ref, rcv, s3_recv, near, out_ref, None)
    greet(True, False)
    hop_first(args)
    deliver(given, rcv, s3_send, s3_recv)
    attend_near(0, q_ref, k_ref, v_ref, near)
    hop_on(args, 1)
    attend_far(0, 0, 2, *far)
    hop_on(args, 2)
    attend_far(0, 2, HG, *far)
    hop_on(args, 3)
    hop_last(args)
    deliver_sent(given, s3_send)


def kernel_attend(
    gate_ref, given, half_ref, weight, other_weight, q_ref, k_ref, v_ref, out_ref,
    rcv, near, half, got, w_own, w_other, total, s3_send, s3_recv, w_sems, half_send, half_recv,
):
    plane, me, tp, _ = place()
    rows = half_ref.shape[0] // 2
    mine = pl.ds(pl.multiple_of(tp * rows, rows), rows)
    theirs = pl.ds(pl.multiple_of((1 - tp) * rows, rows), rows)
    cut = HG * HD

    def swap(source, target, sem):
        return pltpu.make_async_remote_copy(
            src_ref=source,
            dst_ref=target,
            send_sem=half_send.at[sem],
            recv_sem=half_recv.at[sem],
            device_id=(plane * SIDE + me, 1 - tp),
            device_id_type=MESH,
        )

    def head_swap(h):
        return swap(half.at[theirs, columns(h)], got.at[1, :, columns(h)], 1 + h)

    greet(False, True)
    deliver(given, rcv, s3_send, s3_recv)
    first = swap(half_ref.at[theirs], got.at[0], 0)
    first.start()
    loads = [
        pltpu.make_async_copy(weight, w_own, w_sems.at[0]),
        pltpu.make_async_copy(other_weight, w_other, w_sems.at[1]),
    ]
    for load in loads:
        load.start()
    attend_near(1, q_ref, k_ref, v_ref, near)
    for load in loads:
        load.wait()
    first.wait()

    def early(n, carry):
        cols = pl.ds(pl.multiple_of(n * 256, 256), 256)
        total[:, cols] = dot(half_ref[mine], w_own[:cut, cols], ((1,), (0,))) + dot(
            got[0], w_other[:cut, cols], ((1,), (0,))
        )
        return carry

    lax.fori_loop(0, out_ref.shape[1] // 256, early, 0)
    attend_far(
        1, 0, HG, gate_ref, q_ref, rcv, s3_recv, near, half, lambda h: head_swap(h).start()
    )
    for h in range(HG):
        head_swap(h).wait()

    def late(n, carry):
        cols = pl.ds(pl.multiple_of(n * 256, 256), 256)
        mixed = total[:, cols] + dot(half[mine], w_own[cut:, cols], ((1,), (0,)))
        mixed = mixed + dot(got[1], w_other[cut:, cols], ((1,), (0,)))
        out_ref[:, cols] = mixed.astype(BF16)
        return carry

    lax.fori_loop(0, out_ref.shape[1] // 256, late, 0)
    deliver_sent(given, s3_send)


SMEM = pl.BlockSpec(memory_space=pltpu.SMEM)
HBM = pl.BlockSpec(memory_space=pl.ANY)
VMEM = pl.BlockSpec(memory_space=pltpu.VMEM)


def call(kernel, name, number, outs, in_specs, out_specs, scratch, *args):
    return pl.pallas_call(
        kernel,
        out_shape=outs,
        in_specs=in_specs,
        out_specs=out_specs,
        scratch_shapes=scratch,
        compiler_params=pltpu.CompilerParams(
            collective_id=number, has_side_effects=True, vmem_limit_bytes=48 << 20
        ),
        name=name,
    )(*args)


def shape(dims, dtype=BF16):
    return jax.ShapeDtypeStruct(dims, dtype)


def view(rows):
    return rows.reshape(MB, SIDE, ROWS, HL * HD)


def start(mem_keys, mem_values, block_ids, block_home):
    ids = block_ids.transpose(1, 2, 0).reshape(2, HL, TOPK, PLANES * SIDE)
    one = pltpu.SemaphoreType.DMA
    return call(
        kernel_spread, "spread", 0,
        (
            shape((OWN, PIECE, HD)), shape((4, LPAD), jnp.int32),
            shape((HL * TOPK, PLANES * SIDE), jnp.int32), shape((8, 128), F32),
        ),
        [HBM, HBM, VMEM, VMEM], (HBM, VMEM, VMEM, VMEM),
        [pltpu.VMEM((2, PLANES, 4, 256), jnp.int32), pltpu.VMEM((HL, 64, 32), F32), one, one],
        view(mem_keys), view(mem_values), ids, block_home.reshape(8, 128),
    )


def fast_path(own0, lists, dest, gate, mem_keys, mem_values, queries, local_keys, local_values, out_weight):
    tokens = queries.shape[0]
    half = (tokens, HG * HD)
    ring_shape = shape((2 * CSUM, PIECE, HD))
    one = pltpu.SemaphoreType.DMA
    pair, heads, ring = one((2,)), one((HG,)), one((2, 4, 4))
    swaps = one((HG + 1,))
    rcv = pltpu.VMEM((HG, SIDE, TOPK, PIECE, HD), BF16)
    near = pltpu.VMEM(half, F32)
    (lst0,) = pick("pick_first", 0, None, lists, dest, own0, None, None)
    ring0, own1, other_weight = call(
        kernel_ring, "ring", 1, (ring_shape, shape(own0.shape), shape(out_weight.shape)),
        [HBM] * 4, (HBM, HBM, HBM), [one, one, ring, ring, pair],
        view(mem_keys), view(mem_values), out_weight, lst0,
    )
    lst1, given0 = pick("pick_both", 1, 0, lists, dest, own1, own0, ring0)
    ring1, half0 = call(
        kernel_ring_attend, "ring_attend", 2, (ring_shape, shape(half)),
        [SMEM, HBM, HBM, VMEM, VMEM, VMEM], (HBM, VMEM), [rcv, near, ring, ring, one, heads],
        gate, lst1, given0, queries, local_keys, local_values,
    )
    (given1,) = pick("pick_last", None, 1, lists, dest, None, own1, ring1)
    weight = pltpu.VMEM(out_weight.shape, BF16)
    return call(
        kernel_attend, "attend", 3, shape((tokens // 2, out_weight.shape[1])),
        [SMEM, HBM, VMEM, HBM, HBM, VMEM, VMEM, VMEM], VMEM,
        [
            rcv, near, pltpu.VMEM(half, BF16), pltpu.VMEM((2, tokens // 2, HG * HD), BF16),
            weight, weight, pltpu.VMEM((tokens // 2, out_weight.shape[1]), F32),
            one, heads, pair, swaps, swaps,
        ],
        gate, given1, half0, out_weight, other_weight, queries, local_keys, local_values,
    )


def rank_within(owner_row):
    request_count = owner_row.shape[0]
    order_index = jnp.arange(request_count, dtype=jnp.int32)
    earlier = order_index[:, None] > order_index[None, :]
    same_owner = owner_row[:, None] == owner_row[None, :]
    return jnp.sum((same_owner & earlier).astype(jnp.int32), axis=1)


def slow_path(
    gate, mem_keys, mem_values, queries, local_keys, local_values, out_weight, block_ids, block_home
):
    mem_count = lax.axis_size("mem")
    mem_index = lax.axis_index("mem")
    tp_index = lax.axis_index("tp")
    requests = HL * TOPK
    slots = 2
    group_ids = lax.dynamic_slice_in_dim(block_ids, tp_index * HL, HL, 1).reshape(mem_count, requests)
    home_slots = jnp.take(block_home, group_ids, axis=0)
    owners = home_slots // MB
    codes = (home_slots % MB) * HL + jnp.arange(requests, dtype=jnp.int32)[None, :] // TOPK
    own_owners = lax.dynamic_index_in_dim(owners, mem_index, 0, keepdims=False)
    own_codes = lax.dynamic_index_in_dim(codes, mem_index, 0, keepdims=False)
    own_ranks = rank_within(own_owners)
    slot_index = jnp.arange(slots, dtype=jnp.int32)
    owner_index = jnp.arange(mem_count, dtype=jnp.int32)
    matches = (own_owners[None, None, :] == owner_index[:, None, None]) & (
        own_ranks[None, None, :] == slot_index[None, :, None]
    )
    table = jnp.sum(jnp.where(matches, own_codes[None, None, :], 0), axis=2)
    wanted = lax.all_to_all(table, "mem", split_axis=0, concat_axis=0, tiled=True)
    flat_slot = own_owners * slots + own_ranks

    def fetch(rows):
        blocks = rows.reshape(MB, BLK, HL, HD)
        sent = blocks[wanted // HL, :, wanted % HL, :]
        got = lax.all_to_all(sent, "mem", split_axis=0, concat_axis=0, tiled=True)
        far = jnp.take(got.reshape(mem_count * slots, BLK, HD), flat_slot, axis=0)
        return far.reshape(HL, TOPK * BLK, HD)

    positions = jnp.arange(queries.shape[0], dtype=jnp.int32)
    causal = positions[:, None] >= positions[None, :]

    def by_head(x):
        return x.reshape(x.shape[0], HL, HD).transpose(1, 0, 2)

    def one_head(parts):
        q, far_k, far_v, near_k, near_v, g = parts
        remote = dot(softmax_dot(q, far_k, None), far_v, ((1,), (0,)))
        nearby = dot(softmax_dot(q, near_k, causal), near_v, ((1,), (0,)))
        return (g * remote + (1.0 - g) * nearby).astype(BF16)

    out = lax.map(
        one_head,
        (by_head(queries), fetch(mem_keys), fetch(mem_values), by_head(local_keys), by_head(local_values), gate),
    )
    combined = out.transpose(1, 0, 2).reshape(queries.shape)
    partial = jnp.dot(combined, out_weight, preferred_element_type=F32)
    return lax.psum_scatter(partial, "tp", scatter_dimension=0, tiled=True).astype(BF16)


def per_device(
    queries, local_keys, local_values, mem_keys, mem_values, gate_bias, out_weight, block_ids, block_home
):
    gate = jax.nn.sigmoid(gate_bias)
    own0, lists, dest, over = start(mem_keys, mem_values, block_ids, block_home)
    attention = (gate, mem_keys, mem_values, queries, local_keys, local_values, out_weight)
    return lax.cond(
        over[0, 0] <= 0.5,
        lambda: fast_path(own0, lists, dest, *attention),
        lambda: slow_path(*attention, block_ids, block_home),
    )


def solution(mesh):
    in_specs = (
        P("mem", "tp"), P("mem", "tp"), P("mem", "tp"), P("mem", "tp"), P("mem", "tp"),
        P("tp"), P("tp", None), P(), P(),
    )
    return jax.shard_map(
        per_device, mesh=mesh, in_specs=in_specs, out_specs=P(("mem", "tp"), None), check_vma=False
    )
```

time: 578 us -> 322 us (0.56)
  waiting for transfers between devices: 351 us -> 0 us
  Pallas kernels: 0 us -> 301 us
  local copies, waits for them, and re-layouts: 111 us -> 3.71 us
  starting transfers between devices: 37.5 us -> 0 us
  matrix products: 36.8 us -> 0 us
  other arithmetic: 15.1 us -> 0.01 us
    all_to_all x3 -> x0, waiting for transfers between devices: 331 us -> none  [the longest x1 170 us: per_device(): lax.all_to_all(sent_keys, 'mem', split_axis=0, concat_axis=0, tiled=True)]
    pallas_call x0 -> x7, Pallas kernels: none -> 301 us  [the longest x4 277 us: call(): pl.pallas_call(kernel, out_shape=outs, in_specs=in_specs, out_specs=out_s...]
    gather x6 -> x0, local copies, waits for them, and re-layouts: 97.8 us -> none  [the longest x2 65.4 us: per_device(): home_slots = jnp.take(block_home, group_ids, axis=0)]
    all_to_all x3 -> x0, starting transfers between devices: 37.5 us -> none  [the longest x1 16.3 us: per_device(): lax.all_to_all(table, 'mem', split_axis=0, concat_axis=0, tiled=True)]
    dot_general x33 -> x0, matrix products: 36.8 us -> none  [the longest x16 16.3 us: attend(): lax.dot_general(query_head, key_rows, (((1,), (1,)), ((), ())), preferred...]
    reduce_scatter x1 -> x0, waiting for transfers between devices: 19.8 us -> none  [per_device(): lax.psum_scatter(jnp.dot(combined, out_weight, preferred_element_type=jnp...]
    unnamed x40 -> x11, local copies, waits for them, and re-layouts: 9.19 us -> 0.99 us
    reduce_sum x18 -> x0, other arithmetic: 7.93 us -> none  [the longest x16 7.64 us: attend(): jnp.sum(exponent, axis=1, keepdims=True)]
  transfers between devices with their start and end apart: 4 -> 0, of which waited for: 4 -> 0; matrix products, arithmetic and copies ran while one was open for 6% -> 0% of each run, Pallas kernels for 0% -> 0%
where the time goes in v2:
time: 322 us; the launch traced here: 319 us
  Pallas kernels  301 us (93%)
  between operations  14.1 us (4%)
  local copies, waits for them, and re-layouts  3.71 us (1%)
    pallas_call x4, Pallas kernels, call(): pl.pallas_call(kernel, out_shape=outs, in_specs=in_specs, out_specs=out_s...  277 us
    pallas_call x3, Pallas kernels, pick(): pl.pallas_call(kernel, out_shape=tuple(shapes), in_specs=[smem, smem] + [...  23.3 us

profile of v2, /device:TPU:1, one launch (start us, length us, event | category | flops | bytes accessed | tf_op | source)
XLA Modules:
  0.0 318.9 jit_solution(13246474740499980423)
XLA Ops:
  6.5 0.0 copy-start.3
  6.5 0.0 copy-start.11
  6.5 0.0 copy-start.1
  6.5 0.0 copy-start.12
  6.5 0.0 copy-start.5
  6.5 38.0 %spread.1 = (bf16[512,16,128]{2,1,0:T(8,128)(2,1)}, s32[4,384]{1,0:T(4,128)S(1)}, s32[128,128]{1,0:T(8,128)S(1)}, f32[8,128]{1,0:T(8,128)S(1)}) custom-call(bf16[8,16,8,1024]{3,2,1,0:T(8,128)(2,1)} %bitcast.113, bf16[8,16,8,1024]{3,2,1,0:T(8,128)(2,1)} %bitcast.116, s32[2,8,16,128]{3,2,1,0:T(8,128)} %bitcast.127, s32[8,128]{1,0:T(8,128)} %bitcast.110), custom_call_target="tpu_custom_call" | custom-call | tf_op jit(solution)/shard_map/spread/pallas_call | solution.py:551
  44.6 0.0 copy-done.12
  44.6 0.5 slice.3
  45.8 0.0 copy-done.3
  45.8 0.0 copy-done.11
  45.8 0.0 copy-done.1
  45.8 0.0 copy-done.5
  45.8 265.2 %conditional.1 = (bf16[256,2048]{1,0:T(8,128)(2,1)S(1)}) conditional(s32[]{:T(128)} %bitcast.27, (bf16[512,1024]{1,0:T(8,128)(2,1)S(1)}, bf16[1024,1024]{1,0:T(8,128)(2,1)S(1)}, s32[128,16,16]{0,2,1:T(8,128)S(1)}, s32[1024]{0:T(1024)S(1)}, bf16[1024,1024]{1,0:T(8,128)(2,1)}, /*index=5*/bf16[512,1024]{1,0:T(8,128)(2,1)}, ...), branch_computations={%region_0.11_spmd, %region_10.12_spmd} | conditional | flops 2835065856 | bytes 208665152 | solution.py:688
  46.1 0.0 copy-start.2
  46.1 5.8 %pick_first.1.lst = bf16[688,16,128]{2,1,0:T(8,128)(2,1)S(1)} custom-call(s32[4,384]{1,0:T(4,128)S(1)} %get-tuple-element.194.refs_0_, s32[128,128]{1,0:T(8,128)S(1)} %get-tuple-element.195.refs_1_, bf16[512,16,128]{2,1,0:T(8,128)(2,1)} %get-tuple-element.199.refs_2_.refs_3_), custom_call_target="tpu_custom_call" | custom-call | tf_op jit(solution)/shard_map/cond/branch_1_fun/pick_first/pallas_call | solution.py:237
  51.8 0.0 copy-done.2
  51.9 0.0 copy-start.10
  51.9 95.8 %ring.1 = (bf16[1824,16,128]{2,1,0:T(8,128)(2,1)}, bf16[512,16,128]{2,1,0:T(8,128)(2,1)S(1)}, bf16[1024,2048]{1,0:T(8,128)(2,1)}) custom-call(bf16[8,16,8,1024]{3,2,1,0:T(8,128)(2,1)S(1)} %bitcast.115, bf16[8,16,8,1024]{3,2,1,0:T(8,128)(2,1)} %bitcast.118, bf16[1024,2048]{1,0:T(8,128)(2,1)S(1)} %copy-done.2, bf16[688,16,128]{2,1,0:T(8,128)(2,1)S(1)} %pick_first.1.lst), custom_call_target="tpu_custom_call" | custom-call | tf_op jit(solution)/shard_map/cond/branch_1_fun/ring/pallas_call | solution.py:551
  147.6 0.0 copy-done.10
  147.7 0.0 copy-start.7
  147.7 0.0 copy-start.9
  147.7 8.7 %pick_both.1 = (bf16[688,16,128]{2,1,0:T(8,128)(2,1)S(1)}, bf16[1024,16,128]{2,1,0:T(8,128)(2,1)}) custom-call(s32[4,384]{1,0:T(4,128)S(1)} %get-tuple-element.194.refs_0_, s32[128,128]{1,0:T(8,128)S(1)} %get-tuple-element.195.refs_1_, bf16[512,16,128]{2,1,0:T(8,128)(2,1)S(1)} %get-tuple-element.200.refs_2_, bf16[512,16,128]{2,1,0:T(8,128)(2,1)S(1)} %copy-done.10, ...), custom_call_target="tpu_custom_call" | custom-call | tf_op jit(solution)/shard_map/cond/branch_1_fun/pick_both/pallas_call | solution.py:237
  156.4 0.0 copy-done.7
  156.4 0.0 copy-done.9
  156.4 83.5 %ring_attend.1 = (bf16[1824,16,128]{2,1,0:T(8,128)(2,1)}, bf16[512,512]{1,0:T(8,128)(2,1)S(1)}) custom-call(f32[8]{0:T(128)S(1)} %get-tuple-element.193.gate_ref, bf16[688,16,128]{2,1,0:T(8,128)(2,1)S(1)} %get-tuple-element.202.lst, bf16[1024,16,128]{2,1,0:T(8,128)(2,1)} %get-tuple-element.203.given, bf16[512,1024]{1,0:T(8,128)(2,1)S(1)} %get-tuple-element.204.q_ref, ...), custom_call_target="tpu_custom_call" | custom-call | tf_op jit(solution)/shard_map/cond/branch_1_fun/ring_attend/pallas_call | solution.py:551
  239.9 8.8 %pick_last.1.given = bf16[1024,16,128]{2,1,0:T(8,128)(2,1)} custom-call(s32[4,384]{1,0:T(4,128)S(1)} %get-tuple-element.194.refs_0_, s32[128,128]{1,0:T(8,128)S(1)} %get-tuple-element.195.refs_1_, bf16[512,16,128]{2,1,0:T(8,128)(2,1)S(1)} %get-tuple-element.200.refs_2_, bf16[1824,16,128]{2,1,0:T(8,128)(2,1)} %get-tuple-element.207.refs_3_), custom_call_target="tpu_custom_call" | custom-call | tf_op jit(solution)/shard_map/cond/branch_1_fun/pick_last/pallas_call | solution.py:237
  248.8 0.0 copy-start
  248.8 2.2 copy-done
  250.9 60.1 %attend.1 = bf16[256,2048]{1,0:T(8,128)(2,1)S(1)} custom-call(f32[8]{0:T(128)S(1)} %get-tuple-element.193.gate_ref, bf16[1024,16,128]{2,1,0:T(8,128)(2,1)S(1)} %copy-done, bf16[512,512]{1,0:T(8,128)(2,1)S(1)} %get-tuple-element.208.half_ref, bf16[1024,2048]{1,0:T(8,128)(2,1)S(1)} %copy-done.2, bf16[1024,2048]{1,0:T(8,128)(2,1)} %get-tuple-element.209.other_weight, ...), custom_call_target="tpu_custom_call" | custom-call | tf_op jit(solution)/shard_map/cond/branch_1_fun/attend/pallas_call | solution.py:551
  311.1 1.0 copy.81
  (1 shorter events, 0.0 us)
Async XLA Ops:
  6.5 39.3 %copy-start.3 = (bf16[1024,1024]{1,0:T(8,128)(2,1)S(1)}, bf16[1024,1024]{1,0:T(8,128)(2,1)}, u32[]{:S(2)}) copy-start(bf16[1024,1024]{1,0:T(8,128)(2,1)} %param.18) | copy-start | bytes 6291460
  6.5 39.3 %copy-start.11 = (s32[128,16,16]{0,2,1:T(8,128)S(1)}, s32[128,16,16]{0,2,1:T(8,128)}, u32[]{:S(2)}) copy-start(s32[128,16,16]{0,2,1:T(8,128)} %param.22) | copy-start | bytes 393220
  6.5 39.3 %copy-start.1 = (s32[1024]{0:T(1024)S(1)}, s32[1024]{0:T(1024)}, u32[]{:S(2)}) copy-start(s32[1024]{0:T(1024)} %param.23) | copy-start | bytes 12292
  6.5 38.1 %copy-start.12 = (f32[8]{0:T(128)S(1)}, f32[8]{0:T(128)}, u32[]{:S(2)}) copy-start(f32[8]{0:T(128)} %param.20) | copy-start | bytes 100
  6.5 39.3 %copy-start.5 = (bf16[512,1024]{1,0:T(8,128)(2,1)S(1)}, bf16[512,1024]{1,0:T(8,128)(2,1)}, u32[]{:S(2)}) copy-start(bf16[512,1024]{1,0:T(8,128)(2,1)} %param.15) | copy-start | bytes 3145732
  46.1 5.8 %copy-start.2 = (bf16[1024,2048]{1,0:T(8,128)(2,1)S(1)}, bf16[1024,2048]{1,0:T(8,128)(2,1)}, u32[]{:S(2)}) copy-start(bf16[1024,2048]{1,0:T(8,128)(2,1)} %get-tuple-element.198.weight) | copy-start | bytes 12582916 | tf_op jit(solution)/shard_map/cond
  51.9 95.8 %copy-start.10 = (bf16[512,16,128]{2,1,0:T(8,128)(2,1)S(1)}, bf16[512,16,128]{2,1,0:T(8,128)(2,1)}, u32[]{:S(2)}) copy-start(bf16[512,16,128]{2,1,0:T(8,128)(2,1)} %get-tuple-element.199.refs_2_.refs_3_) | copy-start | bytes 6291460 | tf_op jit(solution)/shard_map/cond
  147.7 8.7 %copy-start.7 = (bf16[512,1024]{1,0:T(8,128)(2,1)S(1)}, bf16[512,1024]{1,0:T(8,128)(2,1)}, u32[]{:S(2)}) copy-start(bf16[512,1024]{1,0:T(8,128)(2,1)} %get-tuple-element.205.k_ref) | copy-start | bytes 3145732 | tf_op jit(solution)/shard_map/cond
  147.7 8.7 %copy-start.9 = (bf16[512,1024]{1,0:T(8,128)(2,1)S(1)}, bf16[512,1024]{1,0:T(8,128)(2,1)}, u32[]{:S(2)}) copy-start(bf16[512,1024]{1,0:T(8,128)(2,1)} %get-tuple-element.206.v_ref) | copy-start | bytes 3145732 | tf_op jit(solution)/shard_map/cond
  248.8 2.2 copy-start

commit v3 on v2

--- a/solution.py
+++ b/solution.py
@@ -51,9 +51,34 @@
     return up, down
 
 
-def plan(ids_ref, home_ref, lists_ref, dest_ref, over_ref, rank_s, address_s, plane, tp):
+def find(ids_ref, home_ref, side, h):
     home = home_ref[...]
     home = jnp.concatenate([home >> 5, home & 31], axis=0).astype(F32).astype(BF16)
+    block = ids_ref[side, h]
+    ids = jnp.concatenate([block[q : q + 1] for q in range(TOPK)], axis=1)
+    both = dot(home, hot(iota((128, 2048), 0) == (ids & 127)), ((1,), (0,)))
+    at_hi = iota((8, 2048), 0) == (ids >> 7)
+    pos_hi = jnp.sum(jnp.where(at_hi, both[:8], 0.0), axis=0, keepdims=True).astype(jnp.int32)
+    pos_lo = jnp.sum(jnp.where(at_hi, both[8:], 0.0), axis=0, keepdims=True).astype(jnp.int32)
+    return hot(iota((32, 2048), 0) == pos_hi), pos_lo
+
+
+def plan_requests(ids_ref, home_ref, address_ref, dest_ref, tp):
+    def one_dest(h, carry):
+        by_hi, pos_lo = find(ids_ref, home_ref, tp, h)
+        found = dot(address_ref[h].astype(BF16), by_hi, ((1,), (0,)))
+        at_lo = iota((32, 2048), 0) == pos_lo
+        dest_hi = jnp.sum(jnp.where(at_lo, found[:32], 0.0), axis=0, keepdims=True)
+        dest_lo = jnp.sum(jnp.where(at_lo, found[32:], 0.0), axis=0, keepdims=True)
+        dest = (dest_hi * 32.0 + dest_lo).astype(jnp.int32)
+        rows = jnp.concatenate([dest[:, q * 128 : q * 128 + 128] for q in range(TOPK)], axis=0)
+        dest_ref[pl.ds(pl.multiple_of(h * TOPK, TOPK), TOPK), :] = rows
+        return carry
+
+    lax.fori_loop(0, HL, one_dest, 0)
+
+
+def plan_ring(ids_ref, home_ref, lists_ref, address_ref, over_ref, rank_s, plane, tp):
     lane = iota((1, 2048), 1)
     plane_term = ((lane & 127) >> 4) * 32
     row_plane = iota((32, 256), 0) >> 2
@@ -61,15 +86,6 @@
     dz = ((iota((32, 256), 1) >> 5) - row_plane) & 7
     up, down = ways(dz, even)
     reach = (jnp.where(up, dz, 0), jnp.where(down, 8 - dz, 0))
-
-    def find(side, h):
-        block = ids_ref[side, h]
-        ids = jnp.concatenate([block[q : q + 1] for q in range(TOPK)], axis=1)
-        both = dot(home, hot(iota((128, 2048), 0) == (ids & 127)), ((1,), (0,)))
-        at_hi = iota((8, 2048), 0) == (ids >> 7)
-        pos_hi = jnp.sum(jnp.where(at_hi, both[:8], 0.0), axis=0, keepdims=True).astype(jnp.int32)
-        pos_lo = jnp.sum(jnp.where(at_hi, both[8:], 0.0), axis=0, keepdims=True).astype(jnp.int32)
-        return hot(iota((32, 2048), 0) == pos_hi), pos_lo
 
     r, s = iota((256, 256), 0), iota((256, 256), 1)
     same_group = (r >> 7) == (s >> 7)
@@ -84,7 +100,7 @@
         side = tp if other == 0 else 1 - tp
 
         def one_head(h, far):
-            by_hi, pos_lo = find(side, h)
+            by_hi, pos_lo = find(ids_ref, home_ref, side, h)
             count = dot(by_hi, hot(iota((256, 2048), 0) == plane_term + pos_lo), ((1,), (1,)))
             out = []
             for way in range(2):
@@ -139,20 +155,7 @@
     low = jnp.transpose((address & 31).astype(F32))
     for h in range(HL):
         part = slice(h * 32, h * 32 + 32)
-        address_s[h] = jnp.concatenate([high[part], low[part]], axis=0)
-
-    def one_dest(h, carry):
-        by_hi, pos_lo = find(tp, h)
-        found = dot(address_s[h].astype(BF16), by_hi, ((1,), (0,)))
-        at_lo = iota((32, 2048), 0) == pos_lo
-        dest_hi = jnp.sum(jnp.where(at_lo, found[:32], 0.0), axis=0, keepdims=True)
-        dest_lo = jnp.sum(jnp.where(at_lo, found[32:], 0.0), axis=0, keepdims=True)
-        dest = (dest_hi * 32.0 + dest_lo).astype(jnp.int32)
-        rows = jnp.concatenate([dest[:, q * 128 : q * 128 + 128] for q in range(TOPK)], axis=0)
-        dest_ref[pl.ds(pl.multiple_of(h * TOPK, TOPK), TOPK), :] = rows
-        return carry
-
-    lax.fori_loop(0, HL, one_dest, 0)
+        address_ref[h] = jnp.concatenate([high[part], low[part]], axis=0)
 
 
 def pick_list(g, lists_ref, own, out):
@@ -162,17 +165,14 @@
             out[way * CAPS[0] + j] = own[lists_ref[g * 2 + way, j]]
             return carry
 
-        lax.fori_loop(0, CAPS[0], one, 0, unroll=8)
+        lax.fori_loop(0, CAPS[0], one, 0, unroll=43)
 
 
 def pick_requests(g, r, dest_ref, pool, out):
     column = (lax.axis_index("mem") // SIDE) * SIDE + r
 
-    def one(j, carry):
+    for j in range(SLOTS):
         out[r * SLOTS + j] = pool[dest_ref[g * SLOTS + j, column]]
-        return carry
-
-    lax.fori_loop(0, SLOTS, one, 0, unroll=16)
 
 
 def pick(name, list_group, request_group, lists, dest, own_next, own, ring):
@@ -188,7 +188,7 @@
         own_hbm, ring_hbm = (refs.pop(0), refs.pop(0)) if with_requests else (None, None)
         list_hbm = refs.pop(0) if with_list else None
         given_hbm = refs.pop(0) if with_requests else None
-        in_sem, out_sem = refs.pop(), refs.pop()
+        out_sem, in_sem = refs.pop(), refs.pop()
         if with_list:
             next_v, list_v = refs.pop(0), refs.pop(0)
             next_in = pltpu.make_async_copy(next_hbm, next_v, in_sem.at[0])
@@ -196,9 +196,15 @@
         if with_requests:
             pool_v, given_v = refs.pop(0), refs.pop(0)
             own_in = pltpu.make_async_copy(own_hbm, pool_v.at[pl.ds(0, OWN)], in_sem.at[1])
-            ring_in = pltpu.make_async_copy(ring_hbm, pool_v.at[pl.ds(OWN, 2 * CSUM)], in_sem.at[2])
-            own_in.start()
-            ring_in.start()
+            cut = CSUM // 2
+            ring_in = [
+                pltpu.make_async_copy(
+                    ring_hbm.at[pl.ds(n * cut, cut)], pool_v.at[pl.ds(OWN + n * cut, cut)], in_sem.at[2 + n]
+                )
+                for n in range(4)
+            ]
+            for copy in ring_in + [own_in]:
+                copy.start()
         outs = []
         if with_list:
             next_in.wait()
@@ -206,8 +212,8 @@
             outs.append(pltpu.make_async_copy(list_v, list_hbm, out_sem.at[steps]))
             outs[-1].start()
         if with_requests:
-            own_in.wait()
-            ring_in.wait()
+            for copy in ring_in + [own_in]:
+                copy.wait()
             for step in range(steps):
                 wide = SIDE // steps
 
@@ -239,8 +245,8 @@
         out_shape=tuple(shapes),
         in_specs=[smem, smem] + [hbm] * len(data),
         out_specs=tuple([hbm] * len(shapes)),
-        scratch_shapes=scratch + [pltpu.SemaphoreType.DMA((steps + 1,)), pltpu.SemaphoreType.DMA((3,))],
-        compiler_params=pltpu.CompilerParams(vmem_limit_bytes=48 << 20),
+        scratch_shapes=scratch + [pltpu.SemaphoreType.DMA((6,)), pltpu.SemaphoreType.DMA((steps + 1,))],
+        compiler_params=pltpu.CompilerParams(vmem_limit_bytes=(24 if with_requests else 10) << 20),
         name=name,
     )(lists, dest, *data)
 
@@ -253,12 +259,17 @@
     return plane, me, lax.axis_index("tp"), (above, below)
 
 
+def peer_of(me, k):
+    step = (k * 7) % SIDE
+    return ((me // 4 + step // 4) % 4) * 4 + (me % 4 + step % 4) % 4
+
+
 def greet(ring, partner):
     plane, me, tp, nexts = place()
     barrier = pltpu.get_barrier_semaphore()
 
     def one(k, carry):
-        peer = plane * SIDE + (me + k) % SIDE
+        peer = plane * SIDE + peer_of(me, k)
         pl.semaphore_signal(barrier, inc=1, device_id=(peer, tp), device_id_type=MESH)
         return carry
 
@@ -289,7 +300,7 @@
                 )
 
     def to_peer(k, carry):
-        i = (me + k) % SIDE
+        i = peer_of(me, k)
         for source, target in parts(i):
             pltpu.make_async_remote_copy(
                 src_ref=source,
@@ -356,7 +367,7 @@
     for h in range(HG):
 
         def to_peer(k, carry):
-            i = (me + k) % SIDE
+            i = peer_of(me, k)
             pltpu.make_async_remote_copy(
                 src_ref=given.at[pl.ds(i * SLOTS + h * TOPK, TOPK)],
                 dst_ref=rcv.at[h, me],
@@ -430,22 +441,40 @@
 
 
 def kernel_spread(
-    mem_keys, mem_values, ids_ref, home_ref, own, lists_ref, dest_ref, over_ref, rank_s, address_s, send, recv
+    mem_keys, mem_values, ids_ref, home_ref, own, lists_ref, address_ref, over_ref, rank_s, send, recv
 ):
     plane, _, tp, _ = place()
     greet(False, False)
     spread(0, (mem_keys, mem_values), own, send, recv)
-    plan(ids_ref, home_ref, lists_ref, dest_ref, over_ref, rank_s, address_s, plane, tp)
+    plan_ring(ids_ref, home_ref, lists_ref, address_ref, over_ref, rank_s, plane, tp)
     spread_wait(own, send, recv)
 
 
-def kernel_ring(mem_keys, mem_values, weight, lst, ring, own_next, other_weight, *sems):
-    s1_send, s1_recv, z_send, z_recv, w_sems = sems
+def kernel_ring(
+    mem_keys, mem_values, lst, ids_ref, home_ref, address_ref, ring, own_next, dest_ref, *sems
+):
+    s1_send, s1_recv, z_send, z_recv = sems
+    args = (lst, ring, z_send, z_recv)
+    greet(True, False)
+    hop_first(args)
+    spread(1, (mem_keys, mem_values), own_next, s1_send, s1_recv)
+    for d in range(1, 4):
+        hop_on(args, d)
+    plan_requests(ids_ref, home_ref, address_ref, dest_ref, lax.axis_index("tp"))
+    hop_last(args)
+    spread_wait(own_next, s1_send, s1_recv)
+
+
+def kernel_ring_attend(
+    gate_ref, lst, given, weight, q_ref, k_ref, v_ref, ring, out_ref, other_weight, rcv, near, *sems
+):
+    z_send, z_recv, s3_send, s3_recv, w_sems = sems
     plane, me, tp, _ = place()
     args = (lst, ring, z_send, z_recv)
+    far = (gate_ref, q_ref, rcv, s3_recv, near, out_ref, None)
     greet(True, True)
     hop_first(args)
-    spread(1, (mem_keys, mem_values), own_next, s1_send, s1_recv)
+    deliver(given, rcv, s3_send, s3_recv)
     swap = pltpu.make_async_remote_copy(
         src_ref=weight,
         dst_ref=other_weight,
@@ -455,20 +484,6 @@
         device_id_type=MESH,
     )
     swap.start()
-    for d in range(1, 4):
-        hop_on(args, d)
-    hop_last(args)
-    spread_wait(own_next, s1_send, s1_recv)
-    swap.wait()
-
-
-def kernel_ring_attend(gate_ref, lst, given, q_ref, k_ref, v_ref, ring, out_ref, rcv, near, *sems):
-    z_send, z_recv, s3_send, s3_recv = sems
-    args = (lst, ring, z_send, z_recv)
-    far = (gate_ref, q_ref, rcv, s3_recv, near, out_ref, None)
-    greet(True, False)
-    hop_first(args)
-    deliver(given, rcv, s3_send, s3_recv)
     attend_near(0, q_ref, k_ref, v_ref, near)
     hop_on(args, 1)
     attend_far(0, 0, 2, *far)
@@ -477,6 +492,7 @@
     hop_on(args, 3)
     hop_last(args)
     deliver_sent(given, s3_send)
+    swap.wait()
 
 
 def kernel_attend(
@@ -547,7 +563,7 @@
 VMEM = pl.BlockSpec(memory_space=pltpu.VMEM)
 
 
-def call(kernel, name, number, outs, in_specs, out_specs, scratch, *args):
+def call(kernel, name, number, mib, outs, in_specs, out_specs, scratch, *args):
     return pl.pallas_call(
         kernel,
         out_shape=outs,
@@ -555,7 +571,7 @@
         out_specs=out_specs,
         scratch_shapes=scratch,
         compiler_params=pltpu.CompilerParams(
-            collective_id=number, has_side_effects=True, vmem_limit_bytes=48 << 20
+            collective_id=number, has_side_effects=True, vmem_limit_bytes=mib << 20
         ),
         name=name,
     )(*args)
@@ -569,22 +585,24 @@
     return rows.reshape(MB, SIDE, ROWS, HL * HD)
 
 
-def start(mem_keys, mem_values, block_ids, block_home):
-    ids = block_ids.transpose(1, 2, 0).reshape(2, HL, TOPK, PLANES * SIDE)
+def start(mem_keys, mem_values, ids, home):
     one = pltpu.SemaphoreType.DMA
     return call(
-        kernel_spread, "spread", 0,
+        kernel_spread, "spread", 0, 24,
         (
             shape((OWN, PIECE, HD)), shape((4, LPAD), jnp.int32),
-            shape((HL * TOPK, PLANES * SIDE), jnp.int32), shape((8, 128), F32),
+            shape((HL, 64, 32), F32), shape((8, 128), F32),
         ),
         [HBM, HBM, VMEM, VMEM], (HBM, VMEM, VMEM, VMEM),
-        [pltpu.VMEM((2, PLANES, 4, 256), jnp.int32), pltpu.VMEM((HL, 64, 32), F32), one, one],
-        view(mem_keys), view(mem_values), ids, block_home.reshape(8, 128),
-    )
-
-
-def fast_path(own0, lists, dest, gate, mem_keys, mem_values, queries, local_keys, local_values, out_weight):
+        [pltpu.VMEM((2, PLANES, 4, 256), jnp.int32), one, one],
+        view(mem_keys), view(mem_values), ids, home,
+    )
+
+
+def fast_path(
+    own0, lists, address, ids, home, gate,
+    mem_keys, mem_values, queries, local_keys, local_values, out_weight,
+):
     tokens = queries.shape[0]
     half = (tokens, HG * HD)
     ring_shape = shape((2 * CSUM, PIECE, HD))
@@ -593,22 +611,25 @@
     swaps = one((HG + 1,))
     rcv = pltpu.VMEM((HG, SIDE, TOPK, PIECE, HD), BF16)
     near = pltpu.VMEM(half, F32)
-    (lst0,) = pick("pick_first", 0, None, lists, dest, own0, None, None)
-    ring0, own1, other_weight = call(
-        kernel_ring, "ring", 1, (ring_shape, shape(own0.shape), shape(out_weight.shape)),
-        [HBM] * 4, (HBM, HBM, HBM), [one, one, ring, ring, pair],
-        view(mem_keys), view(mem_values), out_weight, lst0,
+    (lst0,) = pick("pick_first", 0, None, lists, lists, own0, None, None)
+    ring0, own1, dest = call(
+        kernel_ring, "ring", 1, 16,
+        (ring_shape, shape(own0.shape), shape((HL * TOPK, PLANES * SIDE), jnp.int32)),
+        [HBM, HBM, HBM, VMEM, VMEM, VMEM], (HBM, HBM, VMEM), [one, one, ring, ring],
+        view(mem_keys), view(mem_values), lst0, ids, home, address,
     )
     lst1, given0 = pick("pick_both", 1, 0, lists, dest, own1, own0, ring0)
-    ring1, half0 = call(
-        kernel_ring_attend, "ring_attend", 2, (ring_shape, shape(half)),
-        [SMEM, HBM, HBM, VMEM, VMEM, VMEM], (HBM, VMEM), [rcv, near, ring, ring, one, heads],
-        gate, lst1, given0, queries, local_keys, local_values,
+    ring1, half0, other_weight = call(
+        kernel_ring_attend, "ring_attend", 2, 28,
+        (ring_shape, shape(half), shape(out_weight.shape)),
+        [SMEM, HBM, HBM, HBM, VMEM, VMEM, VMEM], (HBM, VMEM, HBM),
+        [rcv, near, ring, ring, one, heads, pair],
+        gate, lst1, given0, out_weight, queries, local_keys, local_values,
     )
     (given1,) = pick("pick_last", None, 1, lists, dest, None, own1, ring1)
     weight = pltpu.VMEM(out_weight.shape, BF16)
     return call(
-        kernel_attend, "attend", 3, shape((tokens // 2, out_weight.shape[1])),
+        kernel_attend, "attend", 3, 40, shape((tokens // 2, out_weight.shape[1])),
         [SMEM, HBM, VMEM, HBM, HBM, VMEM, VMEM, VMEM], VMEM,
         [
             rcv, near, pltpu.VMEM(half, BF16), pltpu.VMEM((2, tokens // 2, HG * HD), BF16),
@@ -683,11 +704,13 @@
     queries, local_keys, local_values, mem_keys, mem_values, gate_bias, out_weight, block_ids, block_home
 ):
     gate = jax.nn.sigmoid(gate_bias)
-    own0, lists, dest, over = start(mem_keys, mem_values, block_ids, block_home)
+    ids = block_ids.transpose(1, 2, 0).reshape(2, HL, TOPK, PLANES * SIDE)
+    home = block_home.reshape(8, 128)
+    own0, lists, address, over = start(mem_keys, mem_values, ids, home)
     attention = (gate, mem_keys, mem_values, queries, local_keys, local_values, out_weight)
     return lax.cond(
         over[0, 0] <= 0.5,
-        lambda: fast_path(own0, lists, dest, *attention),
+        lambda: fast_path(own0, lists, address, ids, home, *attention),
         lambda: slow_path(*attention, block_ids, block_home),
     )
 

time: 322 us -> 302 us (0.938)
  Pallas kernels: 301 us -> 284 us
    pallas_call x4, Pallas kernels: 277 us -> 268 us  [call(): pl.pallas_call(kernel, out_shape=outs, in_specs=in_specs, out_specs=out_s...]
    pallas_call x3, Pallas kernels: 23.3 us -> 16.1 us  [pick(): pl.pallas_call(kernel, out_shape=tuple(shapes), in_specs=[smem, smem] + [...]
where the time goes in v3:
time: 302 us; the launch traced here: 301 us
  Pallas kernels  284 us (94%)
  between operations  14.1 us (5%)
    pallas_call x4, Pallas kernels, call(): pl.pallas_call(kernel, out_shape=outs, in_specs=in_specs, out_specs=out_s...  268 us
    pallas_call x3, Pallas kernels, pick(): pl.pallas_call(kernel, out_shape=tuple(shapes), in_specs=[smem, smem] + [...  16.1 us

profile of v3, /device:TPU:1, one launch (start us, length us, event | category | flops | bytes accessed | tf_op | source)
XLA Modules:
  0.0 301.4 jit_solution(11530131499943570415)
XLA Ops:
  6.5 0.0 copy-start.11
  6.5 0.0 copy-start
  6.5 0.0 copy-start.2
  6.5 0.0 copy-start.13
  6.5 0.0 copy-start.5
  6.5 32.6 %spread.1 = (bf16[512,16,128]{2,1,0:T(8,128)(2,1)}, s32[4,384]{1,0:T(4,128)S(1)}, f32[8,64,32]{2,1,0:T(8,128)}, f32[8,128]{1,0:T(8,128)S(1)}) custom-call(bf16[8,16,8,1024]{3,2,1,0:T(8,128)(2,1)} %bitcast.114, bf16[8,16,8,1024]{3,2,1,0:T(8,128)(2,1)} %bitcast.117, s32[2,8,16,128]{3,2,1,0:T(8,128)} %bitcast.128, s32[8,128]{1,0:T(8,128)} %bitcast.110), custom_call_target="tpu_custom_call" | custom-call | tf_op jit(solution)/shard_map/spread/pallas_call | solution.py:567
  39.1 0.0 copy-done.13
  39.1 0.5 slice.3
  40.3 0.0 copy-done.11
  40.3 0.0 copy-done
  40.3 0.0 copy-done.2
  40.3 0.0 copy-done.5
  40.3 251.9 %conditional.1 = (bf16[256,2048]{1,0:T(8,128)(2,1)}) conditional(s32[]{:T(128)} %bitcast.27, (bf16[512,1024]{1,0:T(8,128)(2,1)S(1)}, bf16[1024,1024]{1,0:T(8,128)(2,1)S(1)}, s32[128,16,16]{0,2,1:T(8,128)S(1)}, s32[1024]{0:T(1024)S(1)}, bf16[1024,1024]{1,0:T(8,128)(2,1)}, /*index=5*/bf16[512,1024]{1,0:T(8,128)(2,1)}, bf16[512,1024]{1,0:T(8,128)(2,1)}, ...), branch_computations={%region_0.11_spmd, %region_10.12_spmd} | conditional | flops 2835065856 | bytes 208665152 | solution.py:711
  40.6 0.0 copy-start.4
  40.6 0.0 copy-start.12
  40.6 4.5 %pick_first.1.lst = bf16[688,16,128]{2,1,0:T(8,128)(2,1)S(1)} custom-call(s32[4,384]{1,0:T(4,128)S(1)} %get-tuple-element.198.refs_0_.refs_1_, s32[4,384]{1,0:T(4,128)S(1)} %get-tuple-element.198.refs_0_.refs_1_, bf16[512,16,128]{2,1,0:T(8,128)(2,1)} %get-tuple-element.201.refs_2_.refs_3_), custom_call_target="tpu_custom_call" | custom-call | tf_op jit(solution)/shard_map/cond/branch_1_fun/pick_first/pallas_call | solution.py:243
  45.1 0.0 copy-start.10
  45.1 0.0 copy-done.4
  45.1 0.0 copy-done.12
  45.1 89.9 %ring.1 = (bf16[1824,16,128]{2,1,0:T(8,128)(2,1)S(1)}, bf16[512,16,128]{2,1,0:T(8,128)(2,1)S(1)}, s32[128,128]{1,0:T(8,128)S(1)}) custom-call(bf16[8,16,8,1024]{3,2,1,0:T(8,128)(2,1)S(1)} %bitcast.116, bf16[8,16,8,1024]{3,2,1,0:T(8,128)(2,1)S(1)} %bitcast.119, bf16[688,16,128]{2,1,0:T(8,128)(2,1)S(1)} %pick_first.1.lst, ...), custom_call_target="tpu_custom_call" | custom-call | tf_op jit(solution)/shard_map/cond/branch_1_fun/ring/pallas_call | solution.py:567
  135.1 0.0 copy-done.10
  135.1 0.0 copy-start.1
  135.1 0.0 copy-start.7
  135.1 0.0 copy-start.9
  135.1 6.9 %pick_both.1 = (bf16[688,16,128]{2,1,0:T(8,128)(2,1)S(1)}, bf16[1024,16,128]{2,1,0:T(8,128)(2,1)S(1)}) custom-call(s32[4,384]{1,0:T(4,128)S(1)} %get-tuple-element.198.refs_0_.refs_1_, s32[128,128]{1,0:T(8,128)S(1)} %get-tuple-element.205.refs_1_, bf16[512,16,128]{2,1,0:T(8,128)(2,1)S(1)} %get-tuple-element.206.refs_2_, ...), custom_call_target="tpu_custom_call" | custom-call | tf_op jit(solution)/shard_map/cond/branch_1_fun/pick_both/pallas_call | solution.py:243
  142.1 0.0 copy-done.1
  142.1 0.0 copy-done.7
  142.1 0.0 copy-done.9
  142.1 83.8 %ring_attend.1 = (bf16[1824,16,128]{2,1,0:T(8,128)(2,1)S(1)}, bf16[512,512]{1,0:T(8,128)(2,1)S(1)}, bf16[1024,2048]{1,0:T(8,128)(2,1)S(1)}) custom-call(f32[8]{0:T(128)S(1)} %get-tuple-element.197.gate_ref, bf16[688,16,128]{2,1,0:T(8,128)(2,1)S(1)} %get-tuple-element.208.lst, bf16[1024,16,128]{2,1,0:T(8,128)(2,1)S(1)} %get-tuple-element.209.given, ...), custom_call_target="tpu_custom_call" | custom-call | tf_op jit(solution)/shard_map/cond/branch_1_fun/ring_attend/pallas_call | solution.py:567
  225.9 4.6 %pick_last.1.given = bf16[1024,16,128]{2,1,0:T(8,128)(2,1)S(1)} custom-call(s32[4,384]{1,0:T(4,128)S(1)} %get-tuple-element.198.refs_0_.refs_1_, s32[128,128]{1,0:T(8,128)S(1)} %get-tuple-element.205.refs_1_, bf16[512,16,128]{2,1,0:T(8,128)(2,1)S(1)} %get-tuple-element.206.refs_2_, bf16[1824,16,128]{2,1,0:T(8,128)(2,1)S(1)} %get-tuple-element.214.refs_3_), custom_call_target="tpu_custom_call" | custom-call | tf_op jit(solution)/shard_map/cond/branch_1_fun/pick_last/pallas_call | solution.py:243
  230.6 61.7 %attend.1 = bf16[256,2048]{1,0:T(8,128)(2,1)} custom-call(f32[8]{0:T(128)S(1)} %get-tuple-element.197.gate_ref, bf16[1024,16,128]{2,1,0:T(8,128)(2,1)S(1)} %pick_last.1.given, bf16[512,512]{1,0:T(8,128)(2,1)S(1)} %get-tuple-element.215.half_ref, bf16[1024,2048]{1,0:T(8,128)(2,1)S(1)} %copy-done.1, bf16[1024,2048]{1,0:T(8,128)(2,1)S(1)} %get-tuple-element.216.other_weight, ...), custom_call_target="tpu_custom_call" | custom-call | tf_op jit(solution)/shard_map/cond/branch_1_fun/attend/pallas_call | solution.py:567
  292.3 2.3 copy.81
  (1 shorter events, 0.0 us)
Async XLA Ops:
  6.5 33.8 %copy-start.11 = (s32[128,16,16]{0,2,1:T(8,128)S(1)}, s32[128,16,16]{0,2,1:T(8,128)}, u32[]{:S(2)}) copy-start(s32[128,16,16]{0,2,1:T(8,128)} %param.22) | copy-start | bytes 393220
  6.5 33.8 %copy-start = (s32[1024]{0:T(1024)S(1)}, s32[1024]{0:T(1024)}, u32[]{:S(2)}) copy-start(s32[1024]{0:T(1024)} %param.23) | copy-start | bytes 12292
  6.5 33.8 %copy-start.2 = (bf16[1024,1024]{1,0:T(8,128)(2,1)S(1)}, bf16[1024,1024]{1,0:T(8,128)(2,1)}, u32[]{:S(2)}) copy-start(bf16[1024,1024]{1,0:T(8,128)(2,1)} %param.18) | copy-start | bytes 6291460
  6.5 32.6 %copy-start.13 = (f32[8]{0:T(128)S(1)}, f32[8]{0:T(128)}, u32[]{:S(2)}) copy-start(f32[8]{0:T(128)} %param.20) | copy-start | bytes 100
  6.5 33.8 %copy-start.5 = (bf16[512,1024]{1,0:T(8,128)(2,1)S(1)}, bf16[512,1024]{1,0:T(8,128)(2,1)}, u32[]{:S(2)}) copy-start(bf16[512,1024]{1,0:T(8,128)(2,1)} %param.15) | copy-start | bytes 3145732
  40.6 4.5 %copy-start.4 = (bf16[1024,1024]{1,0:T(8,128)(2,1)S(1)}, bf16[1024,1024]{1,0:T(8,128)(2,1)}, u32[]{:S(2)}) copy-start(bf16[1024,1024]{1,0:T(8,128)(2,1)} %get-tuple-element.200) | copy-start | bytes 6291460 | tf_op jit(solution)/shard_map/cond
  40.6 4.5 %copy-start.12 = (f32[8,64,32]{2,1,0:T(8,128)S(1)}, f32[8,64,32]{2,1,0:T(8,128)}, u32[]{:S(2)}) copy-start(f32[8,64,32]{2,1,0:T(8,128)} %get-tuple-element.204.address_ref) | copy-start | bytes 196612 | tf_op jit(solution)/shard_map/cond
  45.1 90.0 %copy-start.10 = (bf16[512,16,128]{2,1,0:T(8,128)(2,1)S(1)}, bf16[512,16,128]{2,1,0:T(8,128)(2,1)}, u32[]{:S(2)}) copy-start(bf16[512,16,128]{2,1,0:T(8,128)(2,1)} %get-tuple-element.201.refs_2_.refs_3_) | copy-start | bytes 6291460 | tf_op jit(solution)/shard_map/cond
  135.1 7.0 %copy-start.1 = (bf16[1024,2048]{1,0:T(8,128)(2,1)S(1)}, bf16[1024,2048]{1,0:T(8,128)(2,1)}, u32[]{:S(2)}) copy-start(bf16[1024,2048]{1,0:T(8,128)(2,1)} %get-tuple-element.210.weight) | copy-start | bytes 12582916 | tf_op jit(solution)/shard_map/cond
  135.1 7.0 %copy-start.7 = (bf16[512,1024]{1,0:T(8,128)(2,1)S(1)}, bf16[512,1024]{1,0:T(8,128)(2,1)}, u32[]{:S(2)}) copy-start(bf16[512,1024]{1,0:T(8,128)(2,1)} %get-tuple-element.212.k_ref) | copy-start | bytes 3145732 | tf_op jit(solution)/shard_map/cond
  135.1 7.0 %copy-start.9 = (bf16[512,1024]{1,0:T(8,128)(2,1)S(1)}, bf16[512,1024]{1,0:T(8,128)(2,1)}, u32[]{:S(2)}) copy-start(bf16[512,1024]{1,0:T(8,128)(2,1)} %get-tuple-element.213.v_ref) | copy-start | bytes 3145732 | tf_op jit(solution)/shard_map/cond

commit v4 on v3

--- a/solution.py
+++ b/solution.py
@@ -19,10 +19,10 @@
 MB = 8
 ROWS = BLK // SIDE
 OWN = SIDE * MB * HG
-CAPS = (344, 280, 200, 88)
-OFFS = (0, 344, 624, 824)
-CSUM = 912
-CUTS = (0, 88, 200, 280, 344)
+CAPS = (328, 268, 188, 88)
+OFFS = (0, 328, 596, 784)
+CSUM = 872
+CUTS = (0, 88, 188, 268, 328)
 NPIECE = OWN + 2 * CSUM
 PIECE = 2 * ROWS
 LPAD = 384
@@ -43,12 +43,6 @@
 
 def dot(a, b, dims):
     return lax.dot_general(a, b, (dims, ((), ())), preferred_element_type=F32)
-
-
-def ways(dz, even):
-    up = ((dz >= 1) & (dz <= 3)) | ((dz == 4) & even)
-    down = (dz >= 5) | ((dz == 4) & jnp.logical_not(even))
-    return up, down
 
 
 def find(ids_ref, home_ref, side, h):
@@ -84,8 +78,7 @@
     row_plane = iota((32, 256), 0) >> 2
     even = (iota((32, 256), 1) & 1) == 0
     dz = ((iota((32, 256), 1) >> 5) - row_plane) & 7
-    up, down = ways(dz, even)
-    reach = (jnp.where(up, dz, 0), jnp.where(down, 8 - dz, 0))
+    reach = (jnp.where(dz <= 3, dz, 0), jnp.where(dz >= 5, 8 - dz, 0), jnp.where(dz == 4, 4, 0))
 
     r, s = iota((256, 256), 0), iota((256, 256), 1)
     same_group = (r >> 7) == (s >> 7)
@@ -95,7 +88,7 @@
     rows_before = hot(same_plane & (s < r))
     rows_all = hot(same_plane)
     over = jnp.zeros((32, 256), F32)
-    ranks = []
+    ranks, full = [], []
     for other in range(2):
         side = tp if other == 0 else 1 - tp
 
@@ -103,7 +96,7 @@
             by_hi, pos_lo = find(ids_ref, home_ref, side, h)
             count = dot(by_hi, hot(iota((256, 2048), 0) == plane_term + pos_lo), ((1,), (1,)))
             out = []
-            for way in range(2):
+            for way in range(3):
                 value = jnp.where(count > 0.5, reach[way], 0)
                 for shift in (128, 64, 32):
                     value = jnp.maximum(value, pltpu.roll(value, shift, 1))
@@ -111,7 +104,12 @@
             return tuple(out)
 
         zero = jnp.zeros((32, 256), jnp.int32)
-        far = lax.fori_loop(0, HL, one_head, (zero, zero))
+        up, down, opposite = lax.fori_loop(0, HL, one_head, (zero, zero, zero))
+        upward = (up > down) | ((up == down) & even)
+        far = (
+            jnp.where(upward, jnp.maximum(up, opposite), up),
+            jnp.where(upward, down, jnp.maximum(down, opposite)),
+        )
         levels = jnp.concatenate(
             [jnp.where(far[way] == d, 1.0, 0.0) for way in range(2) for d in (4, 3, 2, 1)], axis=0
         )
@@ -129,6 +127,7 @@
                 base = base + plane_total[part]
                 over = jnp.maximum(over, base - float(CAPS[3 - e]))
             if other == 0:
+                full.append(far[way] == 4)
                 ranks.append(rank.astype(jnp.int32) - 1)
                 for p in range(PLANES):
                     rank_s[way, p] = ranks[way][p * 4 : p * 4 + 4]
@@ -146,7 +145,8 @@
             lists_ref[g * 2 + way : g * 2 + way + 1, :] = index.astype(jnp.int32)
 
     dz = (plane - row_plane) & 7
-    up, down = ways(dz, even)
+    up = ((dz >= 1) & (dz <= 3)) | ((dz == 4) & full[0])
+    down = (dz >= 5) | ((dz == 4) & full[1])
     address = (iota((32, 256), 0) & 3) * 128 + (iota((32, 256), 1) & 127)
     for d in range(1, 5):
         address = jnp.where(up & (dz == d), ranks[0] + (OWN + OFFS[d - 1]), address)
@@ -165,7 +165,7 @@
             out[way * CAPS[0] + j] = own[lists_ref[g * 2 + way, j]]
             return carry
 
-        lax.fori_loop(0, CAPS[0], one, 0, unroll=43)
+        lax.fori_loop(0, CAPS[0], one, 0, unroll=41)
 
 
 def pick_requests(g, r, dest_ref, pool, out):
@@ -496,8 +496,8 @@
 
 
 def kernel_attend(
-    gate_ref, given, half_ref, weight, other_weight, q_ref, k_ref, v_ref, out_ref,
-    rcv, near, half, got, w_own, w_other, total, s3_send, s3_recv, w_sems, half_send, half_recv,
+    gate_ref, given, half_ref, w_own, w_other, q_ref, k_ref, v_ref, out_ref,
+    rcv, near, half, got, total, s3_send, s3_recv, half_send, half_recv,
 ):
     plane, me, tp, _ = place()
     rows = half_ref.shape[0] // 2
@@ -522,15 +522,7 @@
     deliver(given, rcv, s3_send, s3_recv)
     first = swap(half_ref.at[theirs], got.at[0], 0)
     first.start()
-    loads = [
-        pltpu.make_async_copy(weight, w_own, w_sems.at[0]),
-        pltpu.make_async_copy(other_weight, w_other, w_sems.at[1]),
-    ]
-    for load in loads:
-        load.start()
     attend_near(1, q_ref, k_ref, v_ref, near)
-    for load in loads:
-        load.wait()
     first.wait()
 
     def early(n, carry):
@@ -627,14 +619,12 @@
         gate, lst1, given0, out_weight, queries, local_keys, local_values,
     )
     (given1,) = pick("pick_last", None, 1, lists, dest, None, own1, ring1)
-    weight = pltpu.VMEM(out_weight.shape, BF16)
     return call(
-        kernel_attend, "attend", 3, 40, shape((tokens // 2, out_weight.shape[1])),
-        [SMEM, HBM, VMEM, HBM, HBM, VMEM, VMEM, VMEM], VMEM,
+        kernel_attend, "attend", 3, 36, shape((tokens // 2, out_weight.shape[1])),
+        [SMEM, HBM, VMEM, VMEM, VMEM, VMEM, VMEM, VMEM], VMEM,
         [
             rcv, near, pltpu.VMEM(half, BF16), pltpu.VMEM((2, tokens // 2, HG * HD), BF16),
-            weight, weight, pltpu.VMEM((tokens // 2, out_weight.shape[1]), F32),
-            one, heads, pair, swaps, swaps,
+            pltpu.VMEM((tokens // 2, out_weight.shape[1]), F32), one, heads, swaps, swaps,
         ],
         gate, given1, half0, out_weight, other_weight, queries, local_keys, local_values,
     )

time: 302 us -> 296 us (0.980)
  Pallas kernels: 284 us -> 278 us
    pallas_call x4, Pallas kernels: 268 us -> 261 us  [call(): pl.pallas_call(kernel, out_shape=outs, in_specs=in_specs, out_specs=out_s...]
where the time goes in v4:
time: 296 us
  Pallas kernels  278 us (94%)
  between operations  14.1 us (5%)
    pallas_call x4, Pallas kernels, call(): pl.pallas_call(kernel, out_shape=outs, in_specs=in_specs, out_specs=out_s...  261 us
    pallas_call x3, Pallas kernels, pick(): pl.pallas_call(kernel, out_shape=tuple(shapes), in_specs=[smem, smem] + [...  17.3 us

profile of v4, /device:TPU:1, one launch (start us, length us, event | category | flops | bytes accessed | tf_op | source)
XLA Modules:
  0.0 295.6 jit_solution(6579157613917989181)
XLA Ops:
  6.5 0.0 copy-start.11
  6.5 0.0 copy-start
  6.5 0.0 copy-start.2
  6.5 0.0 copy-start.13
  6.5 0.0 copy-start.5
  6.5 32.6 %spread.1 = (bf16[512,16,128]{2,1,0:T(8,128)(2,1)}, s32[4,384]{1,0:T(4,128)S(1)}, f32[8,64,32]{2,1,0:T(8,128)}, f32[8,128]{1,0:T(8,128)S(1)}) custom-call(bf16[8,16,8,1024]{3,2,1,0:T(8,128)(2,1)} %bitcast.114, bf16[8,16,8,1024]{3,2,1,0:T(8,128)(2,1)} %bitcast.117, s32[2,8,16,128]{3,2,1,0:T(8,128)} %bitcast.128, s32[8,128]{1,0:T(8,128)} %bitcast.110), custom_call_target="tpu_custom_call" | custom-call | tf_op jit(solution)/shard_map/spread/pallas_call | solution.py:559
  39.1 0.0 copy-done.13
  39.1 0.5 slice.3
  40.3 0.0 copy-done.11
  40.3 0.0 copy-done
  40.3 0.0 copy-done.2
  40.3 0.0 copy-done.5
  40.3 246.1 %conditional.1 = (bf16[256,2048]{1,0:T(8,128)(2,1)}) conditional(s32[]{:T(128)} %bitcast.27, (bf16[512,1024]{1,0:T(8,128)(2,1)S(1)}, bf16[1024,1024]{1,0:T(8,128)(2,1)S(1)}, s32[128,16,16]{0,2,1:T(8,128)S(1)}, s32[1024]{0:T(1024)S(1)}, bf16[1024,1024]{1,0:T(8,128)(2,1)}, /*index=5*/bf16[512,1024]{1,0:T(8,128)(2,1)}, bf16[512,1024]{1,0:T(8,128)(2,1)}, ...), branch_computations={%region_0.11_spmd, %region_10.12_spmd} | conditional | flops 2835065856 | bytes 208665152 | solution.py:701
  40.6 0.0 copy-start.4
  40.6 0.0 copy-start.12
  40.6 4.2 %pick_first.1.lst = bf16[656,16,128]{2,1,0:T(8,128)(2,1)S(1)} custom-call(s32[4,384]{1,0:T(4,128)S(1)} %get-tuple-element.198.refs_0_.refs_1_, s32[4,384]{1,0:T(4,128)S(1)} %get-tuple-element.198.refs_0_.refs_1_, bf16[512,16,128]{2,1,0:T(8,128)(2,1)} %get-tuple-element.201.refs_2_.refs_3_), custom_call_target="tpu_custom_call" | custom-call | tf_op jit(solution)/shard_map/cond/branch_1_fun/pick_first/pallas_call | solution.py:243
  44.8 0.0 copy-start.10
  44.9 0.0 copy-done.4
  44.9 0.0 copy-done.12
  44.9 86.4 %ring.1 = (bf16[1744,16,128]{2,1,0:T(8,128)(2,1)S(1)}, bf16[512,16,128]{2,1,0:T(8,128)(2,1)S(1)}, s32[128,128]{1,0:T(8,128)S(1)}) custom-call(bf16[8,16,8,1024]{3,2,1,0:T(8,128)(2,1)S(1)} %bitcast.116, bf16[8,16,8,1024]{3,2,1,0:T(8,128)(2,1)S(1)} %bitcast.119, bf16[656,16,128]{2,1,0:T(8,128)(2,1)S(1)} %pick_first.1.lst, ...), custom_call_target="tpu_custom_call" | custom-call | tf_op jit(solution)/shard_map/cond/branch_1_fun/ring/pallas_call | solution.py:559
  131.3 0.0 copy-done.10
  131.3 0.0 copy-start.1
  131.3 0.0 copy-start.7
  131.4 0.0 copy-start.9
  131.4 7.6 %pick_both.1 = (bf16[656,16,128]{2,1,0:T(8,128)(2,1)S(1)}, bf16[1024,16,128]{2,1,0:T(8,128)(2,1)S(1)}) custom-call(s32[4,384]{1,0:T(4,128)S(1)} %get-tuple-element.198.refs_0_.refs_1_, s32[128,128]{1,0:T(8,128)S(1)} %get-tuple-element.205.refs_1_, bf16[512,16,128]{2,1,0:T(8,128)(2,1)S(1)} %get-tuple-element.206.refs_2_, ...), custom_call_target="tpu_custom_call" | custom-call | tf_op jit(solution)/shard_map/cond/branch_1_fun/pick_both/pallas_call | solution.py:243
  138.9 0.0 copy-done.1
  138.9 0.0 copy-done.7
  139.0 0.0 copy-done.9
  139.0 80.3 %ring_attend.1 = (bf16[1744,16,128]{2,1,0:T(8,128)(2,1)S(1)}, bf16[512,512]{1,0:T(8,128)(2,1)S(1)}, bf16[1024,2048]{1,0:T(8,128)(2,1)S(1)}) custom-call(f32[8]{0:T(128)S(1)} %get-tuple-element.197.gate_ref, bf16[656,16,128]{2,1,0:T(8,128)(2,1)S(1)} %get-tuple-element.208.lst, bf16[1024,16,128]{2,1,0:T(8,128)(2,1)S(1)} %get-tuple-element.209.given, ...), custom_call_target="tpu_custom_call" | custom-call | tf_op jit(solution)/shard_map/cond/branch_1_fun/ring_attend/pallas_call | solution.py:559
  219.3 5.5 %pick_last.1.given = bf16[1024,16,128]{2,1,0:T(8,128)(2,1)S(1)} custom-call(s32[4,384]{1,0:T(4,128)S(1)} %get-tuple-element.198.refs_0_.refs_1_, s32[128,128]{1,0:T(8,128)S(1)} %get-tuple-element.205.refs_1_, bf16[512,16,128]{2,1,0:T(8,128)(2,1)S(1)} %get-tuple-element.206.refs_2_, bf16[1744,16,128]{2,1,0:T(8,128)(2,1)S(1)} %get-tuple-element.214.refs_3_), custom_call_target="tpu_custom_call" | custom-call | tf_op jit(solution)/shard_map/cond/branch_1_fun/pick_last/pallas_call | solution.py:243
  224.8 61.7 %attend.1 = bf16[256,2048]{1,0:T(8,128)(2,1)} custom-call(f32[8]{0:T(128)S(1)} %get-tuple-element.197.gate_ref, bf16[1024,16,128]{2,1,0:T(8,128)(2,1)S(1)} %pick_last.1.given, bf16[512,512]{1,0:T(8,128)(2,1)S(1)} %get-tuple-element.215.half_ref, bf16[1024,2048]{1,0:T(8,128)(2,1)S(1)} %copy-done.1, bf16[1024,2048]{1,0:T(8,128)(2,1)S(1)} %get-tuple-element.216.w_other, ...), custom_call_target="tpu_custom_call" | custom-call | tf_op jit(solution)/shard_map/cond/branch_1_fun/attend/pallas_call | solution.py:559
  286.5 2.3 copy.81
  (1 shorter events, 0.0 us)
Async XLA Ops:
  6.5 33.8 %copy-start.11 = (s32[128,16,16]{0,2,1:T(8,128)S(1)}, s32[128,16,16]{0,2,1:T(8,128)}, u32[]{:S(2)}) copy-start(s32[128,16,16]{0,2,1:T(8,128)} %param.22) | copy-start | bytes 393220
  6.5 33.8 %copy-start = (s32[1024]{0:T(1024)S(1)}, s32[1024]{0:T(1024)}, u32[]{:S(2)}) copy-start(s32[1024]{0:T(1024)} %param.23) | copy-start | bytes 12292
  6.5 33.8 %copy-start.2 = (bf16[1024,1024]{1,0:T(8,128)(2,1)S(1)}, bf16[1024,1024]{1,0:T(8,128)(2,1)}, u32[]{:S(2)}) copy-start(bf16[1024,1024]{1,0:T(8,128)(2,1)} %param.18) | copy-start | bytes 6291460
  6.5 32.6 %copy-start.13 = (f32[8]{0:T(128)S(1)}, f32[8]{0:T(128)}, u32[]{:S(2)}) copy-start(f32[8]{0:T(128)} %param.20) | copy-start | bytes 100
  6.5 33.8 %copy-start.5 = (bf16[512,1024]{1,0:T(8,128)(2,1)S(1)}, bf16[512,1024]{1,0:T(8,128)(2,1)}, u32[]{:S(2)}) copy-start(bf16[512,1024]{1,0:T(8,128)(2,1)} %param.15) | copy-start | bytes 3145732
  40.6 4.3 %copy-start.4 = (bf16[1024,1024]{1,0:T(8,128)(2,1)S(1)}, bf16[1024,1024]{1,0:T(8,128)(2,1)}, u32[]{:S(2)}) copy-start(bf16[1024,1024]{1,0:T(8,128)(2,1)} %get-tuple-element.200) | copy-start | bytes 6291460 | tf_op jit(solution)/shard_map/cond
  40.6 4.3 %copy-start.12 = (f32[8,64,32]{2,1,0:T(8,128)S(1)}, f32[8,64,32]{2,1,0:T(8,128)}, u32[]{:S(2)}) copy-start(f32[8,64,32]{2,1,0:T(8,128)} %get-tuple-element.204.address_ref) | copy-start | bytes 196612 | tf_op jit(solution)/shard_map/cond
  44.8 86.5 %copy-start.10 = (bf16[512,16,128]{2,1,0:T(8,128)(2,1)S(1)}, bf16[512,16,128]{2,1,0:T(8,128)(2,1)}, u32[]{:S(2)}) copy-start(bf16[512,16,128]{2,1,0:T(8,128)(2,1)} %get-tuple-element.201.refs_2_.refs_3_) | copy-start | bytes 6291460 | tf_op jit(solution)/shard_map/cond
  131.3 7.6 %copy-start.1 = (bf16[1024,2048]{1,0:T(8,128)(2,1)S(1)}, bf16[1024,2048]{1,0:T(8,128)(2,1)}, u32[]{:S(2)}) copy-start(bf16[1024,2048]{1,0:T(8,128)(2,1)} %get-tuple-element.210.weight.w_own) | copy-start | bytes 12582916 | tf_op jit(solution)/shard_map/cond
  131.3 7.6 %copy-start.7 = (bf16[512,1024]{1,0:T(8,128)(2,1)S(1)}, bf16[512,1024]{1,0:T(8,128)(2,1)}, u32[]{:S(2)}) copy-start(bf16[512,1024]{1,0:T(8,128)(2,1)} %get-tuple-element.212.k_ref) | copy-start | bytes 3145732 | tf_op jit(solution)/shard_map/cond
  131.4 7.6 %copy-start.9 = (bf16[512,1024]{1,0:T(8,128)(2,1)S(1)}, bf16[512,1024]{1,0:T(8,128)(2,1)}, u32[]{:S(2)}) copy-start(bf16[512,1024]{1,0:T(8,128)(2,1)} %get-tuple-element.213.v_ref) | copy-start | bytes 3145732 | tf_op jit(solution)/shard_map/cond
